TPU v7x, 32 devices: a whole 2x2x4 slice. The times are simulated.
32 devices in a mesh: cfg: 2 (over x), sx: 16 (over z, y, core).
Axes of the slice: x: 2, y: 2, z: 4, core: 2. Of those that a mesh axis runs over, the one named last changes fastest.
Arguments:
- eigvecs: bfloat16 [512, 2, 3, 16, 1024], P('cfg', None, None, 'sx'), parts along dimension 0, may hold values from -6 to 6
- link_seed: int32 [6], P('cfg'), parts along dimension 0, may hold values from 1 to 46336
- ownership: int32 [2080], replicated, may hold values from 0 to 2079, each once
Outputs:
- elementals: float32 [4160, 96], P(('cfg', 'sx')), parts along dimension 0
There are 2 independent parts, one for each index of `cfg`. A program takes and returns all parts, laid end to end along the dimension named above; an argument that names none is the same for every part. Nothing has to cross between parts.
Inputs may be any that keep to these rules, and one draw needn't show every extreme that they name: ownership is a permutation of the pair tiles 0 to 2079.
All inputs are finite; a program needn't handle non-finite values.
Results may differ from a plain program's by a relative error of at most 0.0029.
Values may be sent and summed in bfloat16 or wider, within the bound.
A program may use at most 192 MiB of HBM per device.

v0:
```python
import math

import jax
import jax.numpy as jnp
import numpy as np
from jax import lax
from jax.sharding import PartitionSpec as P

TM = 4
NZ = 64


def from_behind(block, axis, distance):
    devices = range(lax.axis_size(axis))
    route = [((i - distance) % len(devices), i) for i in devices]
    return lax.ppermute(block, axis, route)


def scramble(seed_value, site_code):
    modulus = 46337
    low_part = site_code % modulus
    high_part = site_code // modulus
    mixed_value = (seed_value * seed_value + low_part) % modulus
    mixed_value = (mixed_value * mixed_value + high_part * 977 + 31) % modulus
    angles = []
    for angle_index in range(7):
        scrambled = (mixed_value + 5171 * angle_index + 1) % modulus
        scrambled = (scrambled * scrambled + low_part) % modulus
        scrambled = (scrambled * scrambled + 12345) % modulus
        angles.append(scrambled.astype(jnp.float32) * (2.0 * math.pi / modulus) - math.pi)
    return angles


def link_field(seed_value, site_code):
    angles = scramble(seed_value, site_code)
    cos_alpha, sin_alpha = (jnp.cos(angles[0]), jnp.sin(angles[0]))
    cos_beta, sin_beta = (jnp.cos(angles[1]), jnp.sin(angles[1]))
    cos_gamma, sin_gamma = (jnp.cos(angles[2]), jnp.sin(angles[2]))
    rotation = [
        [
            cos_alpha * cos_beta * cos_gamma - sin_alpha * sin_gamma,
            -cos_alpha * cos_beta * sin_gamma - sin_alpha * cos_gamma,
            cos_alpha * sin_beta,
        ],
        [
            sin_alpha * cos_beta * cos_gamma + cos_alpha * sin_gamma,
            -sin_alpha * cos_beta * sin_gamma + cos_alpha * cos_gamma,
            sin_alpha * sin_beta,
        ],
        [-sin_beta * cos_gamma, sin_beta * sin_gamma, cos_beta],
    ]
    phase_left = [angles[3], angles[4], -angles[3] - angles[4]]
    phase_right = [angles[5], angles[6], -angles[5] - angles[6]]
    link_real = jnp.stack(
        [
            jnp.stack(
                [
                    rotation[row_index][column]
                    * jnp.cos(phase_left[row_index] + phase_right[column])
                    for column in range(3)
                ]
            )
            for row_index in range(3)
        ]
    )
    link_imag = jnp.stack(
        [
            jnp.stack(
                [
                    rotation[row_index][column]
                    * jnp.sin(phase_left[row_index] + phase_right[column])
                    for column in range(3)
                ]
            )
            for row_index in range(3)
        ]
    )
    return (link_real, link_imag)


def hop_vectors(link_real, link_imag, vectors):
    real_part = vectors[:, 0].astype(jnp.float32)
    imag_part = vectors[:, 1].astype(jnp.float32)
    out_real = []
    out_imag = []
    for colour in range(3):
        acc_real = jnp.zeros(real_part[:, 0].shape, jnp.float32)
        acc_imag = jnp.zeros(real_part[:, 0].shape, jnp.float32)
        for source in range(3):
            u_real = link_real[colour, source]
            u_imag = link_imag[colour, source]
            acc_real = acc_real + u_real * real_part[:, source] - u_imag * imag_part[:, source]
            acc_imag = acc_imag + u_real * imag_part[:, source] + u_imag * real_part[:, source]
        out_real.append(acc_real)
        out_imag.append(acc_imag)
    return jnp.stack([jnp.stack(out_real, 1), jnp.stack(out_imag, 1)], 1).astype(jnp.bfloat16)


def shift_along_y(vectors):
    return jnp.roll(vectors, -NZ, 4)


def shift_along_z(vectors):
    plane_sites = vectors.shape[4]
    inside = jnp.roll(vectors, -1, 4)
    wrapped = jnp.roll(vectors, NZ - 1, 4)
    at_edge = jnp.arange(plane_sites, dtype=jnp.int32) % NZ == NZ - 1
    return jnp.where(at_edge, wrapped, inside)


def mode_products(left_side, hopped):
    modes = left_side.shape[0]
    lefts = left_side.reshape(2 * modes, -1)
    rights = hopped.reshape(2 * modes, -1)
    blocks = lax.dot_general(
        lefts, rights, (((1,), (1,)), ((), ())), preferred_element_type=jnp.float32
    )
    blocks = blocks.reshape(modes, 2, modes, 2)
    real_part = blocks[:, 0, :, 0] + blocks[:, 1, :, 1]
    imag_part = blocks[:, 0, :, 1] - blocks[:, 1, :, 0]
    return jnp.stack([real_part, imag_part], 0)


def tile_table(products):
    modes = products.shape[2]
    tile_count = modes // TM
    tiles = products.reshape(3, 2, tile_count, TM, tile_count, TM).transpose(2, 4, 0, 1, 3, 5)
    return tiles.reshape(tile_count * tile_count, 6 * TM * TM)


def per_device(eigvecs, link_seed, ownership):
    modes, _, _, layers, plane_sites = eigvecs.shape
    extent_x = layers * lax.axis_size("sx")
    device_index = lax.axis_index("sx")
    global_x = device_index * layers + jnp.arange(layers, dtype=jnp.int32)
    plane_index = jnp.arange(plane_sites, dtype=jnp.int32)
    site_code = global_x[:, None] * plane_sites + plane_index[None, :]
    hop_y = hop_vectors(*link_field(link_seed[1], site_code), shift_along_y(eigvecs))
    hop_z = hop_vectors(*link_field(link_seed[2], site_code), shift_along_z(eigvecs))
    product_y = mode_products(eigvecs, hop_y)
    product_z = mode_products(eigvecs, hop_z)
    upper_face = from_behind(eigvecs, "sx", -1)
    nearest = jnp.concatenate([eigvecs[:, :, :, 1:], upper_face], 3)
    hop_x = hop_vectors(*link_field(link_seed[0], site_code), nearest)
    product_x = mode_products(eigvecs, hop_x)
    products = jnp.stack([product_x, product_y, product_z], 0)
    tile_count = modes // TM
    upper_rows, upper_cols = np.triu_indices(tile_count)
    pair_rows = jnp.asarray((upper_rows * tile_count + upper_cols).astype(np.int32))
    mirror_rows = jnp.asarray((upper_cols * tile_count + upper_rows).astype(np.int32))
    chosen_rows = jnp.take(pair_rows, ownership)
    normalise = 1.0 / math.sqrt(12.0 * extent_x * plane_sites)
    entries = 6 * TM * TM
    chosen_mirror = jnp.take(mirror_rows, ownership)
    both_rows = jnp.stack([chosen_rows, chosen_mirror], 1)
    packed = jnp.take(tile_table(products), both_rows, axis=0).reshape(-1, 2 * entries)
    summed = lax.psum_scatter(packed, "sx", scatter_dimension=0, tiled=True)
    direct = summed[:, :entries].reshape(-1, 3, 2, TM, TM)
    mirror = jnp.swapaxes(summed[:, entries:].reshape(-1, 3, 2, TM, TM), 3, 4)
    real_part = direct[:, :, 0] - mirror[:, :, 0]
    imag_part = direct[:, :, 1] + mirror[:, :, 1]
    return jnp.stack([real_part, imag_part], 2).reshape(-1, entries) * normalise


def solution(mesh):
    return jax.shard_map(
        per_device,
        mesh=mesh,
        in_specs=(P("cfg", None, None, "sx", None), P("cfg"), P()),
        out_specs=P(("cfg", "sx"), None),
        check_vma=False,
    )
```

profile of v0, /device:TPU:0, one launch (start us, length us, event | category | flops | bytes accessed | tf_op | source)
XLA Modules:
  0.0 704.2 jit_solution(16824374799865171374)
XLA Ops:
  6.5 4.6 copy.71
  11.1 5.5 collective-permute-start
  18.5 1.6 cosine_multiply_fusion.19
  20.1 1.6 sine_multiply_fusion.20
  25.6 1.1 sine_multiply_fusion.8
  28.9 1.1 cosine_multiply_fusion.7
  30.0 1.1 sine_multiply_fusion.5
  31.1 1.1 sine_multiply_fusion.6
  33.4 1.4 cosine_multiply_fusion.10
  36.8 1.1 sine_multiply_fusion.17
  40.0 1.1 cosine_multiply_fusion.16
  41.1 1.1 sine_multiply_fusion.14
  42.2 1.1 sine_multiply_fusion.15
  43.3 1.8 slice.588
  45.1 2.0 slice.585
  47.1 1.8 slice.554
  48.9 3.7 slice.587
  52.6 5.6 slice.553
  58.2 4.3 copy.73
  62.9 11.4 %gather_fusion.2 = s32[2080]{0:T(1024)S(1)} fusion(s32[2080]{0:T(1024)S(1)} %copy-done.1, s32[3072]{0:T(1024)S(1)} %pad_clamp_fusion.1), kind=kCustom, calls=%fused_computation.1.clone | custom fusion | bytes 24960 | tf_op jit(solution)/shard_map/jit(_take)/gather | solution.py:154
  74.4 11.4 %gather_fusion.1 = s32[2080]{0:T(1024)S(1)} fusion(s32[2080]{0:T(1024)S(1)} %copy-done, s32[3072]{0:T(1024)S(1)} %pad_clamp_fusion.1), kind=kCustom, calls=%fused_computation.clone | custom fusion | bytes 24960 | tf_op jit(solution)/shard_map/jit(_take)/gather | solution.py:151
  87.0 2.8 fusion.8
  93.1 2.7 copy.79
  95.9 1.8 copy.100
  97.6 4.4 maximum_select_fusion
  106.1 2.7 copy.87
  108.8 1.8 copy.101
  111.0 1.8 copy.99
  112.7 2.0 convolution_bitcast_fusion
  114.7 2.4 convolution_bitcast_fusion.1
  117.8 68.4 %reshape.5098 = f32[256,2,256,2]{3,2,1,0:T(8,128)} reshape(f32[512,512]{1,0:T(8,128)S(1)} %copy.88) | data formatting | bytes 2097152 | tf_op jit(solution)/shard_map/reshape | solution.py:118
  186.1 46.5 %fusion.1 = (f32[256,256]{1,0:T(8,128)S(1)}, f32[256,256]{1,0:T(8,128)S(1)}) fusion(f32[256,2,256,2]{3,2,1,0:T(8,128)} %reshape.5098), kind=kLoop, calls=%fused_computation.6 | loop fusion | flops 131072 | bytes 1572864 | tf_op jit(solution)/shard_map/add | solution.py:119
  232.7 68.4 %reshape.5097 = f32[256,2,256,2]{3,2,1,0:T(8,128)} reshape(f32[512,512]{1,0:T(8,128)S(1)} %copy.80) | data formatting | bytes 2097152 | tf_op jit(solution)/shard_map/reshape | solution.py:118
  301.0 46.7 %fusion.3 = (f32[256,256]{1,0:T(8,128)S(1)}, f32[256,256]{1,0:T(8,128)S(1)}) fusion(f32[256,2,256,2]{3,2,1,0:T(8,128)} %reshape.5097), kind=kLoop, calls=%fused_computation.10 | loop fusion | flops 131072 | bytes 1572864 | tf_op jit(solution)/shard_map/add | solution.py:119
  349.6 10.1 %add.14181 = f32[1,1,64,4,64,4]{5,4,3,2,1,0:T(8,128)} reshape(f32[256,256]{1,0:T(8,128)S(1)} %get-tuple-element.10) | data formatting | bytes 524288 | tf_op jit(solution)/shard_map/add | solution.py:119
  359.7 6.1 copy.89
  365.8 10.0 %sub.671 = f32[1,1,64,4,64,4]{5,4,3,2,1,0:T(8,128)} reshape(f32[256,256]{1,0:T(8,128)S(1)} %get-tuple-element.11) | data formatting | bytes 524288 | tf_op jit(solution)/shard_map/sub | solution.py:120
  375.8 6.1 copy.90
  382.0 10.0 %add.14098 = f32[1,1,64,4,64,4]{5,4,3,2,1,0:T(8,128)} reshape(f32[256,256]{1,0:T(8,128)S(1)} %get-tuple-element.8) | data formatting | bytes 524288 | tf_op jit(solution)/shard_map/add | solution.py:119
  392.0 6.1 copy.81
  398.1 10.0 %sub.649 = f32[1,1,64,4,64,4]{5,4,3,2,1,0:T(8,128)} reshape(f32[256,256]{1,0:T(8,128)S(1)} %get-tuple-element.9) | data formatting | bytes 524288 | tf_op jit(solution)/shard_map/sub | solution.py:120
  408.2 6.3 copy.82
  414.5 1.1 sine_multiply_fusion.26
  417.8 1.1 cosine_multiply_fusion.25
  418.9 1.1 sine_multiply_fusion.23
  420.0 1.1 sine_multiply_fusion.24
  421.4 2.6 fusion.14
  427.3 3.1 copy.72
  430.4 1.8 copy.98
  432.3 1.8 convolution_bitcast_fusion.2
  434.4 68.4 %reshape.5096 = f32[256,2,256,2]{3,2,1,0:T(8,128)} reshape(f32[512,512]{1,0:T(8,128)S(1)} %copy.74) | data formatting | bytes 2097152 | tf_op jit(solution)/shard_map/reshape | solution.py:118
  502.8 46.5 %fusion.5 = (f32[256,256]{1,0:T(8,128)S(1)}, f32[256,256]{1,0:T(8,128)S(1)}) fusion(f32[256,2,256,2]{3,2,1,0:T(8,128)} %reshape.5096), kind=kLoop, calls=%fused_computation.14 | loop fusion | flops 131072 | bytes 1572864 | tf_op jit(solution)/shard_map/add | solution.py:119
  549.3 10.1 %add.14016 = f32[1,1,64,4,64,4]{5,4,3,2,1,0:T(8,128)} reshape(f32[256,256]{1,0:T(8,128)S(1)} %get-tuple-element.6) | data formatting | bytes 524288 | tf_op jit(solution)/shard_map/add | solution.py:119
  559.4 6.3 copy.75
  565.7 10.0 %sub.627 = f32[1,1,64,4,64,4]{5,4,3,2,1,0:T(8,128)} reshape(f32[256,256]{1,0:T(8,128)S(1)} %get-tuple-element.7) | data formatting | bytes 524288 | tf_op jit(solution)/shard_map/sub | solution.py:120
  575.7 6.1 copy.76
  581.8 2.2 maximum_bitcast_fusion
  584.1 1.9 reshape.5099
  586.0 1.8 copy.92
  587.8 8.7 %gather_fusion = f32[4160,96]{1,0:T(8,128)} fusion(f32[4096,96]{1,0:T(8,128)S(1)} %copy.92, s32[5120]{0:T(1024)S(1)} %pad_clamp_fusion), kind=kCustom, calls=%fused_computation.2 | custom fusion | bytes 3211520 | tf_op jit(solution)/shard_map/jit(_take)/gather | solution.py:156
  596.5 3.0 copy.93
  599.6 1.3 broadcast_select_fusion
  602.2 92.9 %all-reduce.3.cloned.1.call-done = f32[2080,192]{0,1:T(8,128)} async-done(((f32[2080,192]{0,1:T(8,128)}), f32[2080,192]{0,1:T(8,128)}) %all-reduce.3.cloned.1.call-update) | async-done | bytes 1597456
  695.1 1.1 constant_dynamic-slice_fusion
  (136 shorter events, 28.8 us)
Async XLA Ops:
  6.5 10.1 %copy-start.14 = (s32[3]{0:T(128)S(1)}, s32[3]{0:T(128)}, u32[]{:S(2)}) copy-start(s32[3]{0:T(128)} %param.8) | copy-start | bytes 40
  6.5 688.6 %all-reduce.3.cloned.1.call-start = ((), (), s32[]{:S(2)}) async-start(), calls=%async_computation | async-start | bytes 3342336
  11.1 410.3 %collective-permute-start = (bf16[256,2,3,1,1024]{4,0,2,3,1:T(8,128)(2,1)}, bf16[256,2,3,1,1024]{4,0,2,3,1:T(8,128)(2,1)}, u32[]{:S(2)}, u32[]{:S(2)}) collective-permute-start(bf16[256,2,3,1,1024]{4,0,2,3,1:T(8,128)(2,1)} %copy.71), channel_id=1, source_target_pairs={{1,0},{2,1},{3,2},{4,3},{5,4},{6,5},{7,6},{8,7},{9,8},{10,9},{11,1... | collective-permute-start | bytes 9437192 | tf_op jit(solution)/shard_map/ppermute | solution.py:16
  52.6 5.7 copy-start.3
  58.2 4.7 copy-start.13
  58.2 4.7 copy-start.1
  62.9 11.4 %copy-start = (s32[2080]{0:T(1024)S(1)}, s32[2080]{0:T(1024)}, u32[]{:S(2)}) copy-start(s32[2080]{0:T(1024)} %constant.353.clone2.1) | copy-start | bytes 24964
  85.8 0.6 copy-start.10
  85.8 0.6 copy-start.8
  95.8 1.8 copy-start.6
  95.9 1.8 copy-start.7
  108.8 2.2 copy-start.2
  112.7 2.0 copy-start.4
  301.0 47.7 %copy-start.9 = (s32[2080]{0:T(1024)S(1)}, s32[2080]{0:T(1024)}, u32[]{:S(2)}) copy-start(s32[2080]{0:T(1024)} %copy-done.8) | copy-start | bytes 24964
  301.0 47.7 %copy-start.11 = (s32[2080]{0:T(1024)S(1)}, s32[2080]{0:T(1024)}, u32[]{:S(2)}) copy-start(s32[2080]{0:T(1024)} %copy-done.10) | copy-start | bytes 24964
  301.0 47.7 %copy-start.12 = (s32[2080,2,1]{0,2,1:T(1,128)S(1)}, s32[2080,2,1]{0,2,1:T(1,128)}, u32[]{:S(2)}) copy-start(s32[2080,2,1]{0,2,1:T(1,128)} %compare_select_fusion) | copy-start | bytes 49924
  408.2 12.9 %copy-start.16 = (f32[1,1,1024]{2,1,0:T(1,128)S(1)}, f32[1,1,1024]{2,1,0:T(1,128)}, u32[]{:S(2)}) copy-start(f32[1,1,1024]{2,1,0:T(1,128)} %get-tuple-element.139) | copy-start | bytes 12292
  408.2 12.9 %copy-start.17 = (f32[1,1,1024]{2,1,0:T(1,128)S(1)}, f32[1,1,1024]{2,1,0:T(1,128)}, u32[]{:S(2)}) copy-start(f32[1,1,1024]{2,1,0:T(1,128)} %get-tuple-element.140) | copy-start | bytes 12292
  408.2 12.9 %copy-start.18 = (f32[1,1,1024]{2,1,0:T(1,128)S(1)}, f32[1,1,1024]{2,1,0:T(1,128)}, u32[]{:S(2)}) copy-start(f32[1,1,1024]{2,1,0:T(1,128)} %get-tuple-element.138) | copy-start | bytes 12292
  408.2 12.9 %copy-start.15 = (f32[1,1,1024]{2,1,0:T(1,128)S(1)}, f32[1,1,1024]{2,1,0:T(1,128)}, u32[]{:S(2)}) copy-start(f32[1,1,1024]{2,1,0:T(1,128)} %get-tuple-element.137) | copy-start | bytes 12292
  430.4 1.9 copy-start.5
  599.6 1.4 copy-start.19
Sparse Core Ops, SparseCore 0:
  601.1 94.0 all-reduce.2
where the time goes:
time: 714 us; the launch traced here: 704 us
  local copies, waits for them, and re-layouts  386 us (54%)
  other arithmetic  194 us (27%)
  waiting for transfers between devices  93 us (13%)
  between operations  19 us (3%)
    reshape x3, local copies, waits for them, and re-layouts, mode_products(): blocks = blocks.reshape(modes, 2, modes, 2)  205 us
    add x3, other arithmetic, mode_products(): real_part = blocks[:, 0, :, 0] + blocks[:, 1, :, 1]  140 us
    unnamed x2, waiting for transfers between devices  93 us
    sub x6, local copies, waits for them, and re-layouts, mode_products(): imag_part = blocks[:, 0, :, 1] - blocks[:, 1, :, 0]  48.7 us
    add x6, local copies, waits for them, and re-layouts, mode_products(): real_part = blocks[:, 0, :, 0] + blocks[:, 1, :, 1]  48.7 us
    mul x27, other arithmetic, link_field(): rotation[row_index][column]  29.8 us
    unnamed x48, local copies, waits for them, and re-layouts  17.6 us
  transfers between devices with their start and end apart: 2, of which 1 were waited for; matrix products, arithmetic and copies ran while one was open for 57% of the time, Pallas kernels for 0%

commit v1 on v0

v1 whole, which is shorter than its diff:
```python
import functools
import math

import jax
import jax.numpy as jnp
from jax import lax
from jax.experimental import pallas as pl
from jax.experimental.pallas import tpu as pltpu
from jax.sharding import PartitionSpec as P

TM = 4
NZ = 64
MODULUS = 46337
LANES = 128
ROWS = 16
MESH = pl.DeviceIdType.MESH
F32 = jnp.float32
BF16 = jnp.bfloat16


def from_behind(block, axis, distance):
    devices = range(lax.axis_size(axis))
    route = [((i - distance) % len(devices), i) for i in devices]
    return lax.ppermute(block, axis, route)


def quotient(value):
    q = jnp.floor(value.astype(F32) * (1.0 / MODULUS)).astype(jnp.int32)
    rest = value - q * MODULUS
    q = jnp.where(rest < 0, q - 1, jnp.where(rest >= MODULUS, q + 1, q))
    return q


def modulo(value):
    return value - quotient(value) * MODULUS


def links(seed, first_site, shape):
    code = (
        first_site
        + lax.broadcasted_iota(jnp.int32, shape, 0) * LANES
        + lax.broadcasted_iota(jnp.int32, shape, 1)
    )
    high = quotient(code)
    low = code - high * MODULUS
    mixed = modulo(seed * seed + low)
    mixed = modulo(mixed * mixed + high * 977 + 31)
    th = []
    for k in range(7):
        g = modulo(mixed + (5171 * k + 1))
        g = modulo(g * g + low)
        g = modulo(g * g + 12345)
        th.append(g.astype(F32) * (2.0 * math.pi / MODULUS) - math.pi)
    ca, sa = jnp.cos(th[0]), jnp.sin(th[0])
    cb, sb = jnp.cos(th[1]), jnp.sin(th[1])
    cg, sg = jnp.cos(th[2]), jnp.sin(th[2])
    rot = [
        [ca * cb * cg - sa * sg, -ca * cb * sg - sa * cg, ca * sb],
        [sa * cb * cg + ca * sg, -sa * cb * sg + ca * cg, sa * sb],
        [-sb * cg, sb * sg, cb],
    ]
    left = [th[3], th[4], -th[3] - th[4]]
    right = [th[5], th[6], -th[5] - th[6]]
    real, imag = [], []
    for r in range(3):
        for c in range(3):
            angle = left[r] + right[c]
            real.append(rot[r][c] * jnp.cos(angle))
            imag.append(rot[r][c] * jnp.sin(angle))
    return real + imag


def fill_hops(u_ref, d, src_ref, h_ref, kind):
    modes, sites = src_ref.shape[1], src_ref.shape[2]
    chunks = sites // LANES
    lane = lax.broadcasted_iota(jnp.int32, (ROWS, LANES), 1)

    def chunk_step(k, carry):
        u = [u_ref[d, e, pl.ds(k, 1), :] for e in range(18)]
        at = pl.ds(pl.multiple_of(k * LANES, LANES), LANES)
        after = pl.ds(pl.multiple_of(lax.rem(k + 1, chunks) * LANES, LANES), LANES)

        def rows_step(g, carry):
            rows = pl.ds(pl.multiple_of(g * ROWS, ROWS), ROWS)
            low_rows = pl.ds(pl.multiple_of(modes + g * ROWS, ROWS), ROWS)
            vec = []
            for q in range(6):
                x = src_ref[q, rows, at].astype(F32)
                if kind == 1:
                    nxt = src_ref[q, rows, after].astype(F32)
                    x = pltpu.roll(jnp.where(lane < NZ, nxt, x), NZ, 1)
                if kind == 2:
                    x = jnp.where(
                        lane % NZ == NZ - 1,
                        pltpu.roll(x, NZ - 1, 1),
                        pltpu.roll(x, LANES - 1, 1),
                    )
                vec.append(x)
            for c in range(3):
                re = im = None
                for s in range(3):
                    ur, ui = u[3 * c + s], u[9 + 3 * c + s]
                    vr, vi = vec[s], vec[3 + s]
                    a = ur * vr - ui * vi
                    b = ur * vi + ui * vr
                    re = a if re is None else re + a
                    im = b if im is None else im + b
                re16, im16 = re.astype(BF16), im.astype(BF16)
                h_ref[c, rows, at] = re16
                h_ref[c, low_rows, at] = im16
                h_ref[3 + c, rows, at] = im16
                h_ref[3 + c, low_rows, at] = -re16
            return carry

        return lax.fori_loop(0, modes // ROWS, rows_step, carry)

    lax.fori_loop(0, chunks, chunk_step, 0)


def pack_products(v_ref, h_ref, w_ref, base):
    modes = v_ref.shape[1]
    half = modes // 2
    total = None
    for q in range(6):
        term = lax.dot_general(
            v_ref[q], h_ref[q], (((1,), (1,)), ((), ())), preferred_element_type=F32
        )
        total = term if total is None else total + term
    re, im = total[:, :modes], total[:, modes:]
    re = re - re.T
    im = im + im.T
    row = lax.broadcasted_iota(jnp.int32, (half, half), 0)
    col = lax.broadcasted_iota(jnp.int32, (half, half), 1)
    re_mix = jnp.where(row < col, re[:half, :half], re[half:, half:])
    w_ref[base] = jnp.where(row == col, im[half:, half:], re_mix)
    w_ref[base + 1] = re[:half, half:]
    w_ref[base + 2] = jnp.where(row <= col, im[:half, :half], im[half:, half:])
    w_ref[base + 3] = im[:half, half:]


def yz_kernel(seed_ref, v_ref, w_ref, ux_ref, u_ref, h_ref):
    sites = v_ref.shape[2]
    shape = (sites // LANES, LANES)
    first = lax.axis_index("sx") * sites
    for d in (1, 2, 0):
        for e, entry in enumerate(links(seed_ref[d], first, shape)):
            if d == 0:
                ux_ref[0, e] = entry
            else:
                u_ref[d - 1, e] = entry
    for d in (0, 1):
        fill_hops(u_ref, d, v_ref, h_ref, d + 1)
        pack_products(v_ref, h_ref, w_ref, 4 * d)


def x_kernel(ux_ref, v_ref, near_ref, w_ref, h_ref):
    fill_hops(ux_ref, 0, near_ref, h_ref, 0)
    pack_products(v_ref, h_ref, w_ref, 0)


def sum_kernel(chips, w_ref, out_ref, got, part, send, came, mine, full, sems):
    me = lax.axis_index("sx")
    cfg = lax.axis_index("cfg")
    core = lax.rem(me, 2)
    chip = me // 2
    other = 1 - core
    partner = (cfg, chip * 2 + other)

    def chip_at(step):
        return lax.rem(chip + step, chips)

    barrier = pltpu.get_barrier_semaphore()
    pl.semaphore_signal(barrier, inc=1, device_id=partner, device_id_type=MESH)
    for step in range(1, chips):
        pl.semaphore_signal(
            barrier, inc=1, device_id=(cfg, chip_at(step) * 2 + core), device_id_type=MESH
        )
    pl.semaphore_wait(barrier, chips)

    halves = pltpu.make_async_remote_copy(
        src_ref=w_ref.at[other],
        dst_ref=got,
        send_sem=sems.at[0, 0],
        recv_sem=sems.at[1, 0],
        device_id=partner,
        device_id_type=MESH,
    )
    halves.start()
    halves.wait()
    part[...] = w_ref[core] + got[...]
    send[...] = part[...].astype(BF16)

    pieces = []
    for step in range(1, chips):
        to = chip_at(step)
        copy = pltpu.make_async_remote_copy(
            src_ref=send.at[to],
            dst_ref=came.at[step],
            send_sem=sems.at[2, step],
            recv_sem=sems.at[3, step],
            device_id=(cfg, to * 2 + core),
            device_id_type=MESH,
        )
        copy.start()
        pieces.append(copy)
    total = part[chip]
    for step in range(1, chips):
        pieces[step - 1].wait_recv()
        total = total + came[step].astype(F32)
    mine[...] = total.astype(BF16)
    full[core, chip] = total.astype(BF16)

    back = []
    for step in range(1, chips):
        copy = pltpu.make_async_remote_copy(
            src_ref=mine,
            dst_ref=full.at[core, chip],
            send_sem=sems.at[4, step],
            recv_sem=sems.at[5, step],
            device_id=(cfg, chip_at(step) * 2 + core),
            device_id_type=MESH,
        )
        copy.start()
        back.append(copy)
    for copy in back:
        copy.wait_recv()
    halves = pltpu.make_async_remote_copy(
        src_ref=full.at[core],
        dst_ref=full.at[core],
        send_sem=sems.at[0, 1],
        recv_sem=sems.at[1, 1],
        device_id=partner,
        device_id_type=MESH,
    )
    halves.start()
    halves.wait()
    for copy in pieces:
        copy.wait_send()
    for copy in back:
        copy.wait_send()
    out_ref[...] = full[...]


def sum_over_sites(w, collective):
    size = lax.axis_size("sx")
    chips = size // 2
    blocks, rows, lanes = w.shape
    piece = blocks * rows // size
    shape = (2, chips, piece, lanes)
    vmem = pl.BlockSpec(memory_space=pltpu.VMEM)
    out = pl.pallas_call(
        functools.partial(sum_kernel, chips),
        out_shape=jax.ShapeDtypeStruct(shape, BF16),
        in_specs=[vmem],
        out_specs=vmem,
        scratch_shapes=[
            pltpu.VMEM(shape[1:], F32),
            pltpu.VMEM(shape[1:], F32),
            pltpu.VMEM(shape[1:], BF16),
            pltpu.VMEM(shape[1:], BF16),
            pltpu.VMEM(shape[2:], BF16),
            pltpu.VMEM(shape, BF16),
            pltpu.SemaphoreType.DMA((6, max(chips, 2))),
        ],
        compiler_params=pltpu.CompilerParams(
            collective_id=collective, has_side_effects=True
        ),
        name="sum_over_sites" + str(collective),
    )(w.reshape(shape))
    return out.reshape(w.shape)


def tiles_kernel(scale, slot_ref, x_ref, yz_ref, out_ref, m_ref):
    half = x_ref.shape[1]
    modes = 2 * half
    tiles = modes // TM
    slots, entries = out_ref.shape
    row = lax.broadcasted_iota(jnp.int32, (half, half), 0)
    col = lax.broadcasted_iota(jnp.int32, (half, half), 1)
    for d in range(3):
        src, base = (x_ref, 0) if d == 0 else (yz_ref, 4 * d - 4)
        re_w = src[base].astype(F32)
        im_w = src[base + 2].astype(F32)
        re_t, im_t = re_w.T, im_w.T
        zero = jnp.zeros_like(re_w)
        re_top = jnp.where(row < col, re_w, jnp.where(row > col, -re_t, zero))
        re_low = jnp.where(row > col, re_w, jnp.where(row < col, -re_t, zero))
        im_top = jnp.where(row <= col, im_w, im_t)
        im_low = jnp.where(row > col, im_w, jnp.where(row < col, im_t, re_w))
        for t, top, low in ((0, re_top, re_low), (1, im_top, im_low)):
            at = (2 * d + t) * modes
            m_ref[:half, at : at + half] = top.astype(BF16)
            m_ref[:half, at + half : at + modes] = src[base + 2 * t + 1]
            m_ref[half:, at : at + half] = zero.astype(BF16)
            m_ref[half:, at + half : at + modes] = low.astype(BF16)
    slot = slot_ref[...]
    mode = lax.broadcasted_iota(jnp.int32, (slots, modes), 1)
    i = mode // TM
    start = i * tiles - (i * (i - 1)) // 2
    in_row = (slot >= start) & (slot < start + tiles - i)
    i_of = jnp.max(jnp.where(in_row, i, 0), axis=1, keepdims=True)
    j_of = slot - (i_of * tiles - (i_of * (i_of - 1)) // 2) + i_of
    in_col = jnp.concatenate([(i == j_of).astype(F32)] * 6, axis=1)
    place_row = lax.broadcasted_iota(jnp.int32, (6 * modes, entries), 0)
    place_col = lax.broadcasted_iota(jnp.int32, (6 * modes, entries), 1)
    target = place_col - (place_row // modes) * (TM * TM) - place_row % TM
    total = jnp.zeros((slots, entries), F32)
    for r in range(TM):
        pick = (mode == i_of * TM + r).astype(F32).astype(BF16)
        rows = jnp.dot(pick, m_ref[...], preferred_element_type=F32)
        place = (target == r * TM).astype(F32).astype(BF16)
        total = total + jnp.dot(
            (rows * in_col).astype(BF16), place, preferred_element_type=F32
        )
    out_ref[...] = total * scale


def per_device(eigvecs, link_seed, ownership):
    modes, _, _, layers, sites = eigvecs.shape
    size = lax.axis_size("sx")
    me = lax.axis_index("sx")
    half = modes // 2
    extent_x = layers * size
    v = eigvecs.transpose(1, 2, 3, 0, 4).reshape(6, modes, sites)
    near = from_behind(v, "sx", -1)
    vmem = pl.BlockSpec(memory_space=pltpu.VMEM)
    link_shape = (1, 18, sites // LANES, LANES)
    w_yz, u_x = pl.pallas_call(
        yz_kernel,
        out_shape=(
            jax.ShapeDtypeStruct((8, half, half), F32),
            jax.ShapeDtypeStruct(link_shape, F32),
        ),
        in_specs=[pl.BlockSpec(memory_space=pltpu.SMEM), vmem],
        out_specs=(vmem, vmem),
        scratch_shapes=[
            pltpu.VMEM((2,) + link_shape[1:], F32),
            pltpu.VMEM((6, 2 * modes, sites), BF16),
        ],
        name="products_yz",
    )(link_seed, v)
    sum_yz = sum_over_sites(w_yz, 0)
    w_x = pl.pallas_call(
        x_kernel,
        out_shape=jax.ShapeDtypeStruct((4, half, half), F32),
        in_specs=[vmem] * 3,
        out_specs=vmem,
        scratch_shapes=[pltpu.VMEM((6, 2 * modes, sites), BF16)],
        name="products_x",
    )(u_x, v, near)
    sum_x = sum_over_sites(w_x, 1)
    slots = ownership.shape[0] // size
    own = lax.dynamic_slice_in_dim(ownership, me * slots, slots).reshape(slots, 1)
    return pl.pallas_call(
        functools.partial(tiles_kernel, 1.0 / math.sqrt(12.0 * extent_x * sites)),
        out_shape=jax.ShapeDtypeStruct((slots, 6 * TM * TM), F32),
        in_specs=[vmem] * 3,
        out_specs=vmem,
        scratch_shapes=[pltpu.VMEM((modes, 6 * modes), BF16)],
        name="own_tiles",
    )(own, sum_x, sum_yz)


def solution(mesh):
    return jax.shard_map(
        per_device,
        mesh=mesh,
        in_specs=(P("cfg", None, None, "sx", None), P("cfg"), P()),
        out_specs=P(("cfg", "sx"), None),
        check_vma=False,
    )
```

time: 714 us -> 89.5 us (0.13); the launches traced: 704 us -> 89.2 us
  local copies, waits for them, and re-layouts: 386 us -> 4.38 us
  other arithmetic: 194 us -> 0 us
  waiting for transfers between devices: 93 us -> 0.01 us
  Pallas kernels: 0 us -> 79.3 us
  between operations: 19 us -> 0.04 us
    reshape x8 -> x1, local copies, waits for them, and re-layouts: 209 us -> 0.74 us  [per_device(): lax.dynamic_slice_in_dim(ownership, me * slots, slots).reshape(slots, 1)]
    add x3 -> x0, other arithmetic: 140 us -> none  [mode_products(): real_part = blocks[:, 0, :, 0] + blocks[:, 1, :, 1]]
    unnamed x2 -> x0, waiting for transfers between devices: 93 us -> none
    pallas_call x0 -> x5, Pallas kernels: none -> 79.3 us  [the longest x1 34.7 us: per_device(): pl.pallas_call(yz_kernel, out_shape=(jax.ShapeDtypeStruct((8, half, half)...]
    sub x6 -> x0, local copies, waits for them, and re-layouts: 48.7 us -> none  [mode_products(): imag_part = blocks[:, 0, :, 1] - blocks[:, 1, :, 0]]
    add x6 -> x0, local copies, waits for them, and re-layouts: 48.7 us -> none  [mode_products(): real_part = blocks[:, 0, :, 0] + blocks[:, 1, :, 1]]
    gather x4 -> x0, local copies, waits for them, and re-layouts: 34.6 us -> none  [the longest x2 11.7 us: per_device(): jnp.take(tile_table(products), both_rows, axis=0).reshape(-1, 2 * entries)]
    mul x28 -> x0, other arithmetic: 29.9 us -> none  [the longest x27 29.8 us: link_field(): rotation[row_index][column]]
  transfers between devices with their start and end apart: 2 -> 1, of which waited for: 1 -> 0; matrix products, arithmetic and copies ran while one was open for 57% -> 2% of each run, Pallas kernels for 0% -> 56%
where the time goes in v1:
time: 89.5 us; the launch traced here: 89.2 us
  Pallas kernels  79.3 us (89%)
  starting transfers between devices  5.53 us (6%)
  local copies, waits for them, and re-layouts  4.38 us (5%)
    pallas_call x1, Pallas kernels, per_device(): pl.pallas_call(yz_kernel, out_shape=(jax.ShapeDtypeStruct((8, half, half)...  34.7 us
    pallas_call x2, Pallas kernels, sum_over_sites(): pl.pallas_call(functools.partial(sum_kernel, chips), out_shape=jax.ShapeD...  31.4 us
    pallas_call x1, Pallas kernels, per_device(): pl.pallas_call(x_kernel, out_shape=jax.ShapeDtypeStruct((4, half, half),...  9.87 us
    ppermute x1, starting transfers between devices, from_behind(): return lax.ppermute(block, axis, route)  5.53 us
    pallas_call x1, Pallas kernels, per_device(): pl.pallas_call(functools.partial(tiles_kernel, 1.0 / math.sqrt(12.0 * ext...  3.25 us
    transpose x1, local copies, waits for them, and re-layouts, per_device(): v = eigvecs.transpose(1, 2, 3, 0, 4).reshape(6, modes, sites)  2.87 us
  transfers between devices with their start and end apart: 1, of which 0 were waited for; matrix products, arithmetic and copies ran while one was open for 2% of the time, Pallas kernels for 56%

profile of v1, /device:TPU:0, one launch (start us, length us, event | category | flops | bytes accessed | tf_op | source)
XLA Modules:
  0.0 89.2 jit_solution(12920872339554004438)
XLA Ops:
  0.0 2.9 %copy.5 = bf16[2,3,1,256,1024]{4,3,1,0,2:T(8,128)(2,1)S(1)} copy(bf16[2,3,1,256,1024]{4,0,2,1,3:T(2,128)(2,1)} %bitcast.10) | data formatting | bytes 6291456 | tf_op jit(solution)/shard_map/transpose | solution.py:324
  2.9 0.0 copy-start
  2.9 5.5 %collective-permute-start = (bf16[6,256,1024]{2,1,0:T(8,128)(2,1)S(1)}, bf16[6,256,1024]{2,1,0:T(8,128)(2,1)}, u32[]{:S(2)}, u32[]{:S(2)}) collective-permute-start(bf16[6,256,1024]{2,1,0:T(8,128)(2,1)S(1)} %bitcast.7), channel_id=1, source_target_pairs={{1,0},{2,1},{3,2},{4,3},{5,4},{6,5},{7,6},{8,7},{9,8},{10,9},{11,1... | collective-permute-start | bytes 9437192 | tf_op jit(solution)/shard_map/ppermute | solution.py:24
  8.4 0.8 dynamic_slice.3
  9.2 0.7 copy.6.slot_ref
  9.9 0.0 copy-done
  9.9 34.7 %products_yz.1 = (f32[8,128,128]{2,1,0:T(8,128)}, f32[1,18,8,128]{3,2,1,0:T(8,128)}) custom-call(s32[3]{0:T(128)} %seed_ref.1, bf16[6,256,1024]{2,1,0:T(8,128)(2,1)} %bitcast.8), custom_call_target="tpu_custom_call" | custom-call | tf_op jit(solution)/shard_map/products_yz/pallas_call | solution.py:328
  44.6 15.6 %sum_over_sites0.1 = bf16[2,8,64,128]{3,2,1,0:T(8,128)(2,1)} custom-call(f32[2,8,64,128]{3,2,1,0:T(8,128)} %bitcast.13), custom_call_target="tpu_custom_call" | custom-call | tf_op jit(solution)/shard_map/sum_over_sites0/pallas_call | solution.py:251
  60.2 0.0 collective-permute-done.near_ref
  60.3 9.9 %products_x.1 = f32[4,128,128]{2,1,0:T(8,128)} custom-call(f32[1,18,8,128]{3,2,1,0:T(8,128)} %get-tuple-element.7.ux_ref, bf16[6,256,1024]{2,1,0:T(8,128)(2,1)} %bitcast.9, bf16[6,256,1024]{2,1,0:T(8,128)(2,1)} %collective-permute-done.near_ref), custom_call_target="tpu_custom_call" | custom-call | tf_op jit(solution)/shard_map/products_x/pallas_call | solution.py:343
  70.1 15.8 %sum_over_sites1.1 = bf16[2,8,32,128]{3,2,1,0:T(8,128)(2,1)} custom-call(f32[2,8,32,128]{3,2,1,0:T(8,128)} %bitcast.12), custom_call_target="tpu_custom_call" | custom-call | tf_op jit(solution)/shard_map/sum_over_sites1/pallas_call | solution.py:251
  86.0 3.2 %own_tiles.1 = f32[130,96]{1,0:T(8,128)} custom-call(s32[130,1]{1,0:T(8,128)} %copy.6.slot_ref, bf16[4,128,128]{2,1,0:T(8,128)(2,1)} %bitcast.14, bf16[8,128,128]{2,1,0:T(8,128)(2,1)} %bitcast.11), custom_call_target="tpu_custom_call" | custom-call | tf_op jit(solution)/shard_map/own_tiles/pallas_call | solution.py:354
Async XLA Ops:
  2.9 7.0 %copy-start = (bf16[2,3,1,256,1024]{4,3,1,0,2:T(8,128)(2,1)}, bf16[2,3,1,256,1024]{4,3,1,0,2:T(8,128)(2,1)S(1)}, u32[]{:S(2)}) copy-start(bf16[2,3,1,256,1024]{4,3,1,0,2:T(8,128)(2,1)S(1)} %copy.5) | copy-start | bytes 9437188
  2.9 57.4 %collective-permute-start = (bf16[6,256,1024]{2,1,0:T(8,128)(2,1)S(1)}, bf16[6,256,1024]{2,1,0:T(8,128)(2,1)}, u32[]{:S(2)}, u32[]{:S(2)}) collective-permute-start(bf16[6,256,1024]{2,1,0:T(8,128)(2,1)S(1)} %bitcast.7), channel_id=1, source_target_pairs={{1,0},{2,1},{3,2},{4,3},{5,4},{6,5},{7,6},{8,7},{9,8},{10,9},{11,1... | collective-permute-start | bytes 9437192 | tf_op jit(solution)/shard_map/ppermute | solution.py:24

commit v2 on v1

v2 whole, which is shorter than its diff:
```python
import functools
import math

import jax
import jax.numpy as jnp
from jax import lax
from jax.experimental import pallas as pl
from jax.experimental.pallas import tpu as pltpu
from jax.sharding import PartitionSpec as P

TM = 4
NZ = 64
MODULUS = 46337
LANES = 128
ROWS = 16
PARTS = 2
LARGE = 32 * 1024 * 1024
SMALL = 8 * 1024 * 1024
MESH = pl.DeviceIdType.MESH
F32 = jnp.float32
BF16 = jnp.bfloat16


def from_behind(block, axis, distance):
    devices = range(lax.axis_size(axis))
    route = [((i - distance) % len(devices), i) for i in devices]
    return lax.ppermute(block, axis, route)


def quotient(value):
    q = jnp.floor(value.astype(F32) * (1.0 / MODULUS)).astype(jnp.int32)
    rest = value - q * MODULUS
    q = jnp.where(rest < 0, q - 1, jnp.where(rest >= MODULUS, q + 1, q))
    return q


def modulo(value):
    return value - quotient(value) * MODULUS


def links(seed, first_site, shape):
    code = (
        first_site
        + lax.broadcasted_iota(jnp.int32, shape, 0) * LANES
        + lax.broadcasted_iota(jnp.int32, shape, 1)
    )
    high = quotient(code)
    low = code - high * MODULUS
    mixed = modulo(seed * seed + low)
    mixed = modulo(mixed * mixed + high * 977 + 31)
    th = []
    for k in range(7):
        g = modulo(mixed + (5171 * k + 1))
        g = modulo(g * g + low)
        g = modulo(g * g + 12345)
        th.append(g.astype(F32) * (2.0 * math.pi / MODULUS) - math.pi)
    ca, sa = jnp.cos(th[0]), jnp.sin(th[0])
    cb, sb = jnp.cos(th[1]), jnp.sin(th[1])
    cg, sg = jnp.cos(th[2]), jnp.sin(th[2])
    rot = [
        [ca * cb * cg - sa * sg, -ca * cb * sg - sa * cg, ca * sb],
        [sa * cb * cg + ca * sg, -sa * cb * sg + ca * cg, sa * sb],
        [-sb * cg, sb * sg, cb],
    ]
    left = [th[3], th[4], -th[3] - th[4]]
    right = [th[5], th[6], -th[5] - th[6]]
    real, imag = [], []
    for r in range(3):
        for c in range(3):
            angle = left[r] + right[c]
            real.append(rot[r][c] * jnp.cos(angle))
            imag.append(rot[r][c] * jnp.sin(angle))
    return real + imag


def shift_plane(v_refs, sv_ref, kind):
    wide = 2 * LANES
    part, sites = v_refs[0].shape[1], v_refs[0].shape[2]
    row = lax.broadcasted_iota(jnp.int32, (wide, wide), 0)
    col = lax.broadcasted_iota(jnp.int32, (wide, wide), 1)
    if kind == 1:
        source = col + NZ
    else:
        source = jnp.where(col % NZ == NZ - 1, col - (NZ - 1), col + 1)
    move = (row == source).astype(F32).astype(BF16)
    carry_in = (row + wide == source).astype(F32).astype(BF16)[:LANES]
    for j, v_ref in enumerate(v_refs):
        rows = slice(j * part, (j + 1) * part)

        def component(q, carry, v_ref=v_ref, rows=rows):
            for at in range(0, sites, wide):
                x = jnp.dot(v_ref[q, :, at : at + wide], move, preferred_element_type=F32)
                if kind == 1:
                    after = (at + wide) % sites
                    x = x + jnp.dot(
                        v_ref[q, :, after : after + LANES],
                        carry_in,
                        preferred_element_type=F32,
                    )
                sv_ref[q, rows, at : at + wide] = x.astype(BF16)
            return carry

        lax.fori_loop(0, 6, component, 0)


def fill_hops(u_ref, d, src_ref, h_ref):
    modes, sites = src_ref.shape[1], src_ref.shape[2]

    def chunk_step(k, carry):
        u = [
            jnp.broadcast_to(u_ref[d, e, pl.ds(k, 1), :], (8, LANES)) for e in range(18)
        ]
        at = pl.ds(pl.multiple_of(k * LANES, LANES), LANES)

        def rows_step(g, carry):
            rows = pl.ds(pl.multiple_of(g * ROWS, ROWS), ROWS)
            vec = [src_ref[q, rows, at].astype(F32) for q in range(6)]
            parts = []
            for lo in (0, 8):
                v = [x[lo : lo + 8] for x in vec]
                out = []
                for c in range(3):
                    re = im = None
                    for s in range(3):
                        ur, ui = u[3 * c + s], u[9 + 3 * c + s]
                        a = ur * v[s] - ui * v[3 + s]
                        b = ur * v[3 + s] + ui * v[s]
                        re = a if re is None else re + a
                        im = b if im is None else im + b
                    out.append((re, im))
                parts.append(out)
            for c in range(3):
                for t in range(2):
                    both = jnp.concatenate([parts[0][c][t], parts[1][c][t]], 0)
                    h_ref[3 * t + c, rows, at] = both.astype(BF16)
            return carry

        return lax.fori_loop(0, modes // ROWS, rows_step, carry, unroll=2)

    lax.fori_loop(0, sites // LANES, chunk_step, 0)


def negate_imag(v_refs, nv_ref):
    part = v_refs[0].shape[1]
    for j, v_ref in enumerate(v_refs):
        for c in range(3):
            nv_ref[c, j * part : (j + 1) * part] = -v_ref[3 + c]


def gram(v_refs, nv_ref, h_ref):
    total = None
    for q in range(6):
        if q < 3:
            tail = [nv_ref[q]]
        else:
            tail = [r[q - 3] for r in v_refs]
        left = jnp.concatenate([r[q] for r in v_refs] + tail, 0)
        term = lax.dot_general(
            left, h_ref[q], (((1,), (1,)), ((), ())), preferred_element_type=F32
        )
        total = term if total is None else total + term
    return total


def pack_products(total, w_ref, base):
    modes = total.shape[0] // 2
    half = modes // 2
    re, im = total[:modes], total[modes:]
    row = lax.broadcasted_iota(jnp.int32, (half, half), 0)
    col = lax.broadcasted_iota(jnp.int32, (half, half), 1)
    re_top = re[:half, :half] - re[:half, :half].T
    re_low = re[half:, half:] - re[half:, half:].T
    im_top = im[:half, :half] + im[:half, :half].T
    im_low = im[half:, half:] + im[half:, half:].T
    re_mix = jnp.where(row < col, re_top, re_low)
    w_ref[base] = jnp.where(row == col, im_low, re_mix)
    w_ref[base + 1] = re[:half, half:] - re[half:, :half].T
    w_ref[base + 2] = jnp.where(row <= col, im_top, im_low)
    w_ref[base + 3] = im[:half, half:] + im[half:, :half].T


def yz_kernel(seed_ref, *refs):
    v_refs, (w_ref, ux_ref, u_ref, sv_ref, h_ref, nv_ref) = refs[:-6], refs[-6:]
    sites = v_refs[0].shape[2]
    shape = (sites // LANES, LANES)
    first = lax.axis_index("sx") * sites
    for d in (1, 2, 0):
        for e, entry in enumerate(links(seed_ref[d], first, shape)):
            if d == 0:
                ux_ref[0, e] = entry
            else:
                u_ref[d - 1, e] = entry
    negate_imag(v_refs, nv_ref)
    for d in (0, 1):
        shift_plane(v_refs, sv_ref, d + 1)
        fill_hops(u_ref, d, sv_ref, h_ref)
        pack_products(gram(v_refs, nv_ref, h_ref), w_ref, 4 * d)


def x_kernel(parts, ux_ref, *refs):
    v_refs, near_ref, rest = refs[:parts], refs[parts], refs[parts + 1 :]
    done_refs, (out_ref, h_ref, nv_ref) = rest[:-3], rest[-3:]
    negate_imag(v_refs, nv_ref)
    fill_hops(ux_ref, 0, near_ref, h_ref)
    total = gram(v_refs, nv_ref, h_ref)
    if len(done_refs) == 0 and out_ref.ndim == 2:
        out_ref[...] = total
    else:
        pack_products(
            jnp.concatenate([r[...] for r in done_refs] + [total], 1), out_ref, 0
        )


def sum_kernel(chips, w_ref, out_ref, got, send, came, mine, full, sems):
    me = lax.axis_index("sx")
    cfg = lax.axis_index("cfg")
    core = lax.rem(me, 2)
    chip = me // 2
    other = 1 - core
    partner = (cfg, chip * 2 + other)

    def chip_at(step):
        return lax.rem(chip + step, chips)

    barrier = pltpu.get_barrier_semaphore()
    pl.semaphore_signal(barrier, inc=1, device_id=partner, device_id_type=MESH)
    for step in range(1, chips):
        pl.semaphore_signal(
            barrier, inc=1, device_id=(cfg, chip_at(step) * 2 + core), device_id_type=MESH
        )
    pl.semaphore_wait(barrier, chips)

    def copy_to(src, dst, row, step, device):
        return pltpu.make_async_remote_copy(
            src_ref=src,
            dst_ref=dst,
            send_sem=sems.at[row, step],
            recv_sem=sems.at[row + 1, step],
            device_id=device,
            device_id_type=MESH,
        )

    def same_core(step):
        return (cfg, chip_at(step) * 2 + core)

    order = list(range(1, chips)) + [0]
    halves = {}
    for step in order:
        to = chip_at(step)
        halves[step] = copy_to(w_ref.at[other, to], got.at[to], 0, step, partner)
        halves[step].start()
    pieces = {}
    for step in order[:-1]:
        to = chip_at(step)
        halves[step].wait_recv()
        send[to] = (w_ref[core, to] + got[to]).astype(BF16)
        pieces[step] = copy_to(send.at[to], came.at[step], 2, step, same_core(step))
        pieces[step].start()
    halves[0].wait_recv()
    total = w_ref[core, chip] + got[chip]
    for step in order[:-1]:
        pieces[step].wait_recv()
        total = total + came[step].astype(F32)
    mine[...] = total.astype(BF16)
    full[core, chip] = total.astype(BF16)

    back = {}
    for step in order[:-1]:
        back[step] = copy_to(mine, full.at[core, chip], 4, step, same_core(step))
        back[step].start()
    passed = [copy_to(mine, full.at[core, chip], 6, 0, partner)]
    passed[0].start()
    for step in order[:-1]:
        origin = lax.rem(chip + chips - step, chips)
        back[step].wait_recv()
        passed.append(
            copy_to(full.at[core, origin], full.at[core, origin], 6, step, partner)
        )
        passed[-1].start()
    for copy in passed:
        copy.wait()
    for step in order:
        halves[step].wait_send()
    for step in order[:-1]:
        pieces[step].wait_send()
        back[step].wait_send()
    out_ref[...] = full[...]


def sum_over_sites(w, collective):
    size = lax.axis_size("sx")
    chips = size // 2
    blocks, rows, lanes = w.shape
    piece = blocks * rows // size
    shape = (2, chips, piece, lanes)
    vmem = pl.BlockSpec(memory_space=pltpu.VMEM)
    out = pl.pallas_call(
        functools.partial(sum_kernel, chips),
        out_shape=jax.ShapeDtypeStruct(shape, BF16),
        in_specs=[vmem],
        out_specs=vmem,
        scratch_shapes=[
            pltpu.VMEM(shape[1:], F32),
            pltpu.VMEM(shape[1:], BF16),
            pltpu.VMEM(shape[1:], BF16),
            pltpu.VMEM(shape[2:], BF16),
            pltpu.VMEM(shape, BF16),
            pltpu.SemaphoreType.DMA((8, chips)),
        ],
        compiler_params=pltpu.CompilerParams(
            collective_id=collective, has_side_effects=True, vmem_limit_bytes=SMALL
        ),
        name="sum_over_sites" + str(collective),
    )(w.reshape(shape))
    return out.reshape(w.shape)


def tiles_kernel(directions, scale, slot_ref, src_ref, *refs):
    out_ref, m_ref = refs[-2:]
    half = src_ref.shape[1]
    modes = 2 * half
    tiles = modes // TM
    count = len(directions)
    slots, entries = out_ref.shape
    row = lax.broadcasted_iota(jnp.int32, (half, half), 0)
    col = lax.broadcasted_iota(jnp.int32, (half, half), 1)
    for n in range(count):
        base = 4 * n
        re_w = src_ref[base].astype(F32)
        im_w = src_ref[base + 2].astype(F32)
        re_t, im_t = re_w.T, im_w.T
        zero = jnp.zeros_like(re_w)
        re_top = jnp.where(row < col, re_w, jnp.where(row > col, -re_t, zero))
        re_low = jnp.where(row > col, re_w, jnp.where(row < col, -re_t, zero))
        im_top = jnp.where(row <= col, im_w, im_t)
        im_low = jnp.where(row > col, im_w, jnp.where(row < col, im_t, re_w))
        for t, top, low in ((0, re_top, re_low), (1, im_top, im_low)):
            at = (2 * n + t) * modes
            m_ref[:half, at : at + half] = top.astype(BF16)
            m_ref[:half, at + half : at + modes] = src_ref[base + 2 * t + 1]
            m_ref[half:, at : at + half] = zero.astype(BF16)
            m_ref[half:, at + half : at + modes] = low.astype(BF16)
    slot = slot_ref[...]
    mode = lax.broadcasted_iota(jnp.int32, (slots, modes), 1)
    i = mode // TM
    start = i * tiles - (i * (i - 1)) // 2
    in_row = (slot >= start) & (slot < start + tiles - i)
    i_of = jnp.max(jnp.where(in_row, i, 0), axis=1, keepdims=True)
    j_of = slot - (i_of * tiles - (i_of * (i_of - 1)) // 2) + i_of
    in_col = jnp.concatenate([(i == j_of).astype(F32)] * (2 * count), axis=1)
    place_row = lax.broadcasted_iota(jnp.int32, (2 * count * modes, entries), 0)
    place_col = lax.broadcasted_iota(jnp.int32, (2 * count * modes, entries), 1)
    first = 2 * directions[0] * TM * TM
    target = place_col - first - (place_row // modes) * (TM * TM) - place_row % TM
    total = refs[0][...] if len(refs) == 3 else jnp.zeros((slots, entries), F32)
    for r in range(TM):
        pick = (mode == i_of * TM + r).astype(F32).astype(BF16)
        rows = jnp.dot(pick, m_ref[...], preferred_element_type=F32)
        place = (target == r * TM).astype(F32).astype(BF16)
        total = total + jnp.dot(
            (rows * in_col).astype(BF16), place, preferred_element_type=F32
        )
    out_ref[...] = total * scale


def per_device(eigvecs, link_seed, ownership):
    modes, _, _, layers, sites = eigvecs.shape
    size = lax.axis_size("sx")
    me = lax.axis_index("sx")
    half = modes // 2
    part = modes // PARTS
    extent_x = layers * size
    v = [
        eigvecs[j * part : (j + 1) * part].transpose(1, 2, 3, 0, 4).reshape(6, part, sites)
        for j in range(PARTS)
    ]
    near = [from_behind(block, "sx", -1) for block in v]
    slots = ownership.shape[0] // size
    own = lax.dynamic_slice_in_dim(ownership, me * slots, slots).reshape(slots, 1)
    scale = 1.0 / math.sqrt(12.0 * extent_x * sites)
    vmem = pl.BlockSpec(memory_space=pltpu.VMEM)
    link_shape = (1, 18, sites // LANES, LANES)
    plane = (6, modes, sites)
    negated = pltpu.VMEM((3, modes, sites), BF16)
    large = pltpu.CompilerParams(vmem_limit_bytes=LARGE)
    small = pltpu.CompilerParams(vmem_limit_bytes=SMALL)

    def own_tiles(directions, factor, summed, *added):
        wide = 2 * len(directions) * modes
        return pl.pallas_call(
            functools.partial(tiles_kernel, directions, factor),
            out_shape=jax.ShapeDtypeStruct((slots, 6 * TM * TM), F32),
            in_specs=[vmem] * (2 + len(added)),
            out_specs=vmem,
            scratch_shapes=[pltpu.VMEM((modes, wide), BF16)],
            compiler_params=small,
            name="own_tiles" + str(directions[0]),
        )(own, summed, *added)

    w_yz, u_x = pl.pallas_call(
        yz_kernel,
        out_shape=(
            jax.ShapeDtypeStruct((8, half, half), F32),
            jax.ShapeDtypeStruct(link_shape, F32),
        ),
        in_specs=[pl.BlockSpec(memory_space=pltpu.SMEM)] + [vmem] * PARTS,
        out_specs=(vmem, vmem),
        scratch_shapes=[
            pltpu.VMEM((2,) + link_shape[1:], F32),
            pltpu.VMEM(plane, BF16),
            pltpu.VMEM(plane, BF16),
            negated,
        ],
        compiler_params=large,
        name="products_yz",
    )(link_seed, *v)
    yz = own_tiles((1, 2), 1.0, sum_over_sites(w_yz, 0))
    done = []
    for j in range(PARTS):
        last = j == PARTS - 1
        shape = (4, half, half) if last else (2 * modes, part)
        operands = [u_x, *v, near[j]] + (done if last else [])
        done.append(
            pl.pallas_call(
                functools.partial(x_kernel, PARTS),
                out_shape=jax.ShapeDtypeStruct(shape, F32),
                in_specs=[vmem] * len(operands),
                out_specs=vmem,
                scratch_shapes=[pltpu.VMEM((6, part, sites), BF16), negated],
                compiler_params=large,
                name="products_x" + str(j),
            )(*operands)
        )
    return own_tiles((0,), scale, sum_over_sites(done[-1], 1), yz)


def solution(mesh):
    return jax.shard_map(
        per_device,
        mesh=mesh,
        in_specs=(P("cfg", None, None, "sx", None), P("cfg"), P()),
        out_specs=P(("cfg", "sx"), None),
        check_vma=False,
    )
```

time: 89.5 us -> 83.3 us (0.931)
  Pallas kernels: 79.3 us -> 71 us
  local copies, waits for them, and re-layouts: 4.38 us -> 5.66 us
    pallas_call x1, Pallas kernels: 34.7 us -> 18.6 us  [per_device(): pl.pallas_call(yz_kernel, out_shape=(jax.ShapeDtypeStruct((8, half, half)...]
    pallas_call x2, Pallas kernels: 31.4 us -> 39 us  [sum_over_sites(): pl.pallas_call(functools.partial(sum_kernel, chips), out_shape=jax.ShapeD...]
    transpose x1 -> x3, local copies, waits for them, and re-layouts: 2.87 us -> 4.78 us  [per_device(): eigvecs[j * part:(j + 1) * part].transpose(1, 2, 3, 0, 4)]
    ppermute x1 -> x2, starting transfers between devices: 5.53 us -> 6.25 us  [from_behind(): return lax.ppermute(block, axis, route)]
    pallas_call x2 -> x4, Pallas kernels: 13.1 us -> 13.5 us  [the longest x2 10.3 us: per_device(): pl.pallas_call(functools.partial(x_kernel, PARTS), out_shape=jax.ShapeDty...]
  transfers between devices with their start and end apart: 1 -> 2, of which waited for: 0 -> 0; matrix products, arithmetic and copies ran while one was open for 2% -> 2% of each run, Pallas kernels for 56% -> 62%
where the time goes in v2:
time: 83.3 us; the launch traced here: 83 us
  Pallas kernels  71 us (85%)
  starting transfers between devices  6.25 us (8%)
  local copies, waits for them, and re-layouts  5.66 us (7%)
    pallas_call x2, Pallas kernels, sum_over_sites(): pl.pallas_call(functools.partial(sum_kernel, chips), out_shape=jax.ShapeD...  39 us
    pallas_call x1, Pallas kernels, per_device(): pl.pallas_call(yz_kernel, out_shape=(jax.ShapeDtypeStruct((8, half, half)...  18.6 us
    pallas_call x2, Pallas kernels, per_device(): pl.pallas_call(functools.partial(x_kernel, PARTS), out_shape=jax.ShapeDty...  10.3 us
    ppermute x2, starting transfers between devices, from_behind(): return lax.ppermute(block, axis, route)  6.25 us
    transpose x3, local copies, waits for them, and re-layouts, per_device(): eigvecs[j * part:(j + 1) * part].transpose(1, 2, 3, 0, 4)  4.78 us
    pallas_call x2, Pallas kernels, own_tiles(): pl.pallas_call(functools.partial(tiles_kernel, directions, factor), out_s...  3.16 us
  transfers between devices with their start and end apart: 2, of which 0 were waited for; matrix products, arithmetic and copies ran while one was open for 2% of the time, Pallas kernels for 62%

profile of v2, /device:TPU:0, one launch (start us, length us, event | category | flops | bytes accessed | tf_op | source)
XLA Modules:
  0.0 83.0 jit_solution(7815795117254019484)
XLA Ops:
  0.0 3.9 %slice_bitcast_fusion = (bf16[2,3,1,128,1024]{4,0,2,1,3:T(2,128)(2,1)S(1)}, bf16[2,3,1,128,1024]{4,0,2,1,3:T(2,128)(2,1)S(1)}) fusion(bf16[256,2,3,1,1024]{4,1,3,2,0:T(2,128)(2,1)} %param.3), kind=kLoop, calls=%fused_computation | loop fusion | bytes 6291456 | tf_op jit(solution)/shard_map/transpose | solution.py:374
  3.9 0.5 copy.6
  4.3 5.5 %collective-permute-start.1 = (bf16[6,128,1024]{2,1,0:T(8,128)(2,1)S(1)}, bf16[6,128,1024]{2,1,0:T(8,128)(2,1)}, u32[]{:S(2)}, u32[]{:S(2)}) collective-permute-start(bf16[6,128,1024]{2,1,0:T(8,128)(2,1)S(1)} %bitcast.11), channel_id=1, source_target_pairs={{1,0},{2,1},{3,2},{4,3},{5,4},{6,5},{7,6},{8,7},{9,8},{10,9},{11,1... | collective-permute-start | bytes 4718600 | tf_op jit(solution)/shard_map/ppermute | solution.py:27
  9.9 0.0 copy-start
  9.9 0.5 copy.7
  10.3 0.7 collective-permute-start
  11.1 0.8 dynamic_slice.3
  11.8 0.1 copy.9.slot_ref
  11.9 0.0 copy-done
  12.0 18.6 %products_yz.1 = (f32[8,128,128]{2,1,0:T(8,128)S(1)}, f32[1,18,8,128]{3,2,1,0:T(8,128)S(1)}) custom-call(s32[3]{0:T(128)S(1)} %copy-done, bf16[6,128,1024]{2,1,0:T(8,128)(2,1)S(1)} %bitcast.12, bf16[6,128,1024]{2,1,0:T(8,128)(2,1)S(1)} %bitcast.16), custom_call_target="tpu_custom_call" | custom-call | tf_op jit(solution)/shard_map/products_yz/pallas_call | solution.py:400
  30.5 26.3 %sum_over_sites0.1 = bf16[2,8,64,128]{3,2,1,0:T(8,128)(2,1)S(1)} custom-call(f32[2,8,64,128]{3,2,1,0:T(8,128)S(1)} %bitcast.21), custom_call_target="tpu_custom_call" | custom-call | tf_op jit(solution)/shard_map/sum_over_sites0/pallas_call | solution.py:297
  56.8 1.4 %own_tiles1.1.refs_0_ = f32[130,96]{1,0:T(8,128)S(1)} custom-call(s32[130,1]{1,0:T(8,128)S(1)} %copy.9.slot_ref, bf16[8,128,128]{2,1,0:T(8,128)(2,1)S(1)} %bitcast.19), custom_call_target="tpu_custom_call" | custom-call | tf_op jit(solution)/shard_map/own_tiles1/pallas_call | solution.py:390
  58.2 0.0 collective-permute-done.1.refs_2_
  58.2 5.1 %products_x0.1.refs_3_ = f32[512,128]{1,0:T(8,128)S(1)} custom-call(f32[1,18,8,128]{3,2,1,0:T(8,128)S(1)} %get-tuple-element.7.ux_ref, bf16[6,128,1024]{2,1,0:T(8,128)(2,1)S(1)} %bitcast.13, bf16[6,128,1024]{2,1,0:T(8,128)(2,1)S(1)} %bitcast.17, bf16[6,128,1024]{2,1,0:T(8,128)(2,1)} %collective-permute-done.1.refs_2_), custom_call_target="tpu_custom_call" | custom-call | tf_op jit(solution)/shard_map/products_x0/pallas_call | solution.py:424
  63.3 0.0 collective-permute-done.refs_2_
  63.3 5.2 %products_x1.1 = f32[4,128,128]{2,1,0:T(8,128)S(1)} custom-call(f32[1,18,8,128]{3,2,1,0:T(8,128)S(1)} %get-tuple-element.7.ux_ref, bf16[6,128,1024]{2,1,0:T(8,128)(2,1)S(1)} %bitcast.14, bf16[6,128,1024]{2,1,0:T(8,128)(2,1)S(1)} %bitcast.18, bf16[6,128,1024]{2,1,0:T(8,128)(2,1)} %collective-permute-done.refs_2_, f32[512,128]{1,0:T(8,128)S(1)} %products_x0.1.refs_3_), custom_call_target="tpu_custom_call" | custom-call | tf_op jit(solution)/shard_map/products_x1/pallas_call | solution.py:424
  68.5 12.7 %sum_over_sites1.1 = bf16[2,8,32,128]{3,2,1,0:T(8,128)(2,1)S(1)} custom-call(f32[2,8,32,128]{3,2,1,0:T(8,128)S(1)} %bitcast.20), custom_call_target="tpu_custom_call" | custom-call | tf_op jit(solution)/shard_map/sum_over_sites1/pallas_call | solution.py:297
  81.2 1.8 %own_tiles0.1 = f32[130,96]{1,0:T(8,128)} custom-call(s32[130,1]{1,0:T(8,128)S(1)} %copy.9.slot_ref, bf16[4,128,128]{2,1,0:T(8,128)(2,1)S(1)} %bitcast.22, f32[130,96]{1,0:T(8,128)S(1)} %own_tiles1.1.refs_0_), custom_call_target="tpu_custom_call" | custom-call | tf_op jit(solution)/shard_map/own_tiles0/pallas_call | solution.py:390
Async XLA Ops:
  4.3 53.9 %collective-permute-start.1 = (bf16[6,128,1024]{2,1,0:T(8,128)(2,1)S(1)}, bf16[6,128,1024]{2,1,0:T(8,128)(2,1)}, u32[]{:S(2)}, u32[]{:S(2)}) collective-permute-start(bf16[6,128,1024]{2,1,0:T(8,128)(2,1)S(1)} %bitcast.11), channel_id=1, source_target_pairs={{1,0},{2,1},{3,2},{4,3},{5,4},{6,5},{7,6},{8,7},{9,8},{10,9},{11,1... | collective-permute-start | bytes 4718600 | tf_op jit(solution)/shard_map/ppermute | solution.py:27
  9.9 2.1 %copy-start = (s32[3]{0:T(128)S(1)}, s32[3]{0:T(128)}, u32[]{:S(2)}) copy-start(s32[3]{0:T(128)} %seed_ref.1) | copy-start | bytes 40
  10.3 53.0 %collective-permute-start = (bf16[6,128,1024]{2,1,0:T(8,128)(2,1)S(1)}, bf16[6,128,1024]{2,1,0:T(8,128)(2,1)}, u32[]{:S(2)}, u32[]{:S(2)}) collective-permute-start(bf16[6,128,1024]{2,1,0:T(8,128)(2,1)S(1)} %bitcast.15), channel_id=1, source_target_pairs={{1,0},{2,1},{3,2},{4,3},{5,4},{6,5},{7,6},{8,7},{9,8},{10,9},{11,1... | collective-permute-start | bytes 4718600 | tf_op jit(solution)/shard_map/ppermute | solution.py:27

commit v3 on v2

--- a/solution.py
+++ b/solution.py
@@ -13,7 +13,7 @@
 MODULUS = 46337
 LANES = 128
 ROWS = 16
-PARTS = 2
+PARTS = 4
 LARGE = 32 * 1024 * 1024
 SMALL = 8 * 1024 * 1024
 MESH = pl.DeviceIdType.MESH
@@ -211,71 +211,88 @@
         )
 
 
-def sum_kernel(chips, w_ref, out_ref, got, send, came, mine, full, sems):
+def copy_to(src, dst, sems, row, step, device):
+    return pltpu.make_async_remote_copy(
+        src_ref=src,
+        dst_ref=dst,
+        send_sem=sems.at[row, step],
+        recv_sem=sems.at[row + 1, step],
+        device_id=device,
+        device_id_type=MESH,
+    )
+
+
+def core_sum_kernel(w_ref, out_ref, got, sems):
+    me = lax.axis_index("sx")
+    core = lax.rem(me, 2)
+    partner = (lax.axis_index("cfg"), (me // 2) * 2 + 1 - core)
+    barrier = pltpu.get_barrier_semaphore()
+    pl.semaphore_signal(barrier, inc=1, device_id=partner, device_id_type=MESH)
+    pl.semaphore_wait(barrier, 1)
+    copy = copy_to(w_ref.at[1 - core], got, sems, 0, 0, partner)
+    copy.start()
+    copy.wait()
+    out_ref[...] = (w_ref[core] + got[...]).astype(BF16)
+
+
+def sum_kernel(chips, w_ref, yz_ref, x_out, yz_out, got, send, came, mine, full, sems):
     me = lax.axis_index("sx")
     cfg = lax.axis_index("cfg")
     core = lax.rem(me, 2)
     chip = me // 2
     other = 1 - core
     partner = (cfg, chip * 2 + other)
+    rows = w_ref.shape[2]
 
     def chip_at(step):
         return lax.rem(chip + step, chips)
+
+    def same_core(step):
+        return (cfg, chip_at(step) * 2 + core)
 
     barrier = pltpu.get_barrier_semaphore()
     pl.semaphore_signal(barrier, inc=1, device_id=partner, device_id_type=MESH)
     for step in range(1, chips):
         pl.semaphore_signal(
-            barrier, inc=1, device_id=(cfg, chip_at(step) * 2 + core), device_id_type=MESH
+            barrier, inc=1, device_id=same_core(step), device_id_type=MESH
         )
     pl.semaphore_wait(barrier, chips)
 
-    def copy_to(src, dst, row, step, device):
-        return pltpu.make_async_remote_copy(
-            src_ref=src,
-            dst_ref=dst,
-            send_sem=sems.at[row, step],
-            recv_sem=sems.at[row + 1, step],
-            device_id=device,
-            device_id_type=MESH,
-        )
-
-    def same_core(step):
-        return (cfg, chip_at(step) * 2 + core)
-
     order = list(range(1, chips)) + [0]
-    halves = {}
+    halves, pieces, back = {}, {}, {}
     for step in order:
         to = chip_at(step)
-        halves[step] = copy_to(w_ref.at[other, to], got.at[to], 0, step, partner)
+        halves[step] = copy_to(w_ref.at[other, to], got.at[to], sems, 0, step, partner)
         halves[step].start()
-    pieces = {}
     for step in order[:-1]:
         to = chip_at(step)
+        send[to, rows:] = yz_ref[to]
         halves[step].wait_recv()
-        send[to] = (w_ref[core, to] + got[to]).astype(BF16)
-        pieces[step] = copy_to(send.at[to], came.at[step], 2, step, same_core(step))
+        send[to, :rows] = (w_ref[core, to] + got[to]).astype(BF16)
+        pieces[step] = copy_to(
+            send.at[to], came.at[step], sems, 2, step, same_core(step)
+        )
         pieces[step].start()
     halves[0].wait_recv()
-    total = w_ref[core, chip] + got[chip]
+    total = jnp.concatenate(
+        [w_ref[core, chip] + got[chip], yz_ref[chip].astype(F32)], 0
+    )
     for step in order[:-1]:
         pieces[step].wait_recv()
         total = total + came[step].astype(F32)
     mine[...] = total.astype(BF16)
     full[core, chip] = total.astype(BF16)
 
-    back = {}
     for step in order[:-1]:
-        back[step] = copy_to(mine, full.at[core, chip], 4, step, same_core(step))
+        back[step] = copy_to(mine, full.at[core, chip], sems, 4, step, same_core(step))
         back[step].start()
-    passed = [copy_to(mine, full.at[core, chip], 6, 0, partner)]
+    passed = [copy_to(mine, full.at[core, chip], sems, 6, 0, partner)]
     passed[0].start()
     for step in order[:-1]:
         origin = lax.rem(chip + chips - step, chips)
+        block = full.at[core, origin]
         back[step].wait_recv()
-        passed.append(
-            copy_to(full.at[core, origin], full.at[core, origin], 6, step, partner)
-        )
+        passed.append(copy_to(block, block, sems, 6, step, partner))
         passed[-1].start()
     for copy in passed:
         copy.wait()
@@ -284,48 +301,75 @@
     for step in order[:-1]:
         pieces[step].wait_send()
         back[step].wait_send()
-    out_ref[...] = full[...]
-
-
-def sum_over_sites(w, collective):
+    x_out[...] = full[:, :, :rows]
+    yz_out[...] = full[:, :, rows:]
+
+
+def split_rows(w):
     size = lax.axis_size("sx")
-    chips = size // 2
     blocks, rows, lanes = w.shape
-    piece = blocks * rows // size
-    shape = (2, chips, piece, lanes)
+    return w.reshape(2, size // 2, blocks * rows // size, lanes)
+
+
+def sum_over_cores(w):
+    parts = split_rows(w)
     vmem = pl.BlockSpec(memory_space=pltpu.VMEM)
-    out = pl.pallas_call(
-        functools.partial(sum_kernel, chips),
-        out_shape=jax.ShapeDtypeStruct(shape, BF16),
+    return pl.pallas_call(
+        core_sum_kernel,
+        out_shape=jax.ShapeDtypeStruct(parts.shape[1:], BF16),
         in_specs=[vmem],
         out_specs=vmem,
         scratch_shapes=[
-            pltpu.VMEM(shape[1:], F32),
-            pltpu.VMEM(shape[1:], BF16),
-            pltpu.VMEM(shape[1:], BF16),
-            pltpu.VMEM(shape[2:], BF16),
-            pltpu.VMEM(shape, BF16),
+            pltpu.VMEM(parts.shape[1:], F32),
+            pltpu.SemaphoreType.DMA((2, 1)),
+        ],
+        compiler_params=pltpu.CompilerParams(
+            collective_id=0, has_side_effects=True, vmem_limit_bytes=SMALL
+        ),
+        name="sum_over_cores",
+    )(parts)
+
+
+def sum_over_sites(w, part_yz):
+    parts = split_rows(w)
+    _, chips, rows, lanes = parts.shape
+    rows_yz = part_yz.shape[1]
+    both = (chips, rows + rows_yz, lanes)
+    vmem = pl.BlockSpec(memory_space=pltpu.VMEM)
+    x, yz = pl.pallas_call(
+        functools.partial(sum_kernel, chips),
+        out_shape=(
+            jax.ShapeDtypeStruct((2, chips, rows, lanes), BF16),
+            jax.ShapeDtypeStruct((2, chips, rows_yz, lanes), BF16),
+        ),
+        in_specs=[vmem] * 2,
+        out_specs=(vmem, vmem),
+        scratch_shapes=[
+            pltpu.VMEM((chips, rows, lanes), F32),
+            pltpu.VMEM(both, BF16),
+            pltpu.VMEM(both, BF16),
+            pltpu.VMEM(both[1:], BF16),
+            pltpu.VMEM((2,) + both, BF16),
             pltpu.SemaphoreType.DMA((8, chips)),
         ],
         compiler_params=pltpu.CompilerParams(
-            collective_id=collective, has_side_effects=True, vmem_limit_bytes=SMALL
+            collective_id=1, has_side_effects=True, vmem_limit_bytes=SMALL
         ),
-        name="sum_over_sites" + str(collective),
-    )(w.reshape(shape))
-    return out.reshape(w.shape)
-
-
-def tiles_kernel(directions, scale, slot_ref, src_ref, *refs):
-    out_ref, m_ref = refs[-2:]
-    half = src_ref.shape[1]
+        name="sum_over_sites",
+    )(parts, part_yz)
+    return x.reshape(w.shape), yz.reshape(-1, *w.shape[1:])
+
+
+def tiles_kernel(scale, slot_ref, x_ref, yz_ref, out_ref, m_ref):
+    half = x_ref.shape[1]
     modes = 2 * half
     tiles = modes // TM
-    count = len(directions)
+    count = 3
     slots, entries = out_ref.shape
     row = lax.broadcasted_iota(jnp.int32, (half, half), 0)
     col = lax.broadcasted_iota(jnp.int32, (half, half), 1)
     for n in range(count):
-        base = 4 * n
+        src_ref, base = (x_ref, 0) if n == 0 else (yz_ref, 4 * n - 4)
         re_w = src_ref[base].astype(F32)
         im_w = src_ref[base + 2].astype(F32)
         re_t, im_t = re_w.T, im_w.T
@@ -348,19 +392,18 @@
     i_of = jnp.max(jnp.where(in_row, i, 0), axis=1, keepdims=True)
     j_of = slot - (i_of * tiles - (i_of * (i_of - 1)) // 2) + i_of
     in_col = jnp.concatenate([(i == j_of).astype(F32)] * (2 * count), axis=1)
-    place_row = lax.broadcasted_iota(jnp.int32, (2 * count * modes, entries), 0)
-    place_col = lax.broadcasted_iota(jnp.int32, (2 * count * modes, entries), 1)
-    first = 2 * directions[0] * TM * TM
-    target = place_col - first - (place_row // modes) * (TM * TM) - place_row % TM
-    total = refs[0][...] if len(refs) == 3 else jnp.zeros((slots, entries), F32)
+    wide = -(-entries // LANES) * LANES
+    place_row = lax.broadcasted_iota(jnp.int32, (2 * count * modes, wide), 0)
+    place_col = lax.broadcasted_iota(jnp.int32, (2 * count * modes, wide), 1)
+    target = (place_row // modes) * (TM * TM) + place_row % TM
+    place = (target == place_col).astype(F32).astype(BF16)
+    total = jnp.zeros((slots, wide), F32)
     for r in range(TM):
         pick = (mode == i_of * TM + r).astype(F32).astype(BF16)
         rows = jnp.dot(pick, m_ref[...], preferred_element_type=F32)
-        place = (target == r * TM).astype(F32).astype(BF16)
-        total = total + jnp.dot(
-            (rows * in_col).astype(BF16), place, preferred_element_type=F32
-        )
-    out_ref[...] = total * scale
+        found = jnp.dot((rows * in_col).astype(BF16), place, preferred_element_type=F32)
+        total = total + (found if r == 0 else pltpu.roll(found, TM * r, 1))
+    out_ref[...] = total[:, :entries] * scale
 
 
 def per_device(eigvecs, link_seed, ownership):
@@ -385,18 +428,6 @@
     large = pltpu.CompilerParams(vmem_limit_bytes=LARGE)
     small = pltpu.CompilerParams(vmem_limit_bytes=SMALL)
 
-    def own_tiles(directions, factor, summed, *added):
-        wide = 2 * len(directions) * modes
-        return pl.pallas_call(
-            functools.partial(tiles_kernel, directions, factor),
-            out_shape=jax.ShapeDtypeStruct((slots, 6 * TM * TM), F32),
-            in_specs=[vmem] * (2 + len(added)),
-            out_specs=vmem,
-            scratch_shapes=[pltpu.VMEM((modes, wide), BF16)],
-            compiler_params=small,
-            name="own_tiles" + str(directions[0]),
-        )(own, summed, *added)
-
     w_yz, u_x = pl.pallas_call(
         yz_kernel,
         out_shape=(
@@ -414,7 +445,7 @@
         compiler_params=large,
         name="products_yz",
     )(link_seed, *v)
-    yz = own_tiles((1, 2), 1.0, sum_over_sites(w_yz, 0))
+    part_yz = sum_over_cores(w_yz)
     done = []
     for j in range(PARTS):
         last = j == PARTS - 1
@@ -431,7 +462,16 @@
                 name="products_x" + str(j),
             )(*operands)
         )
-    return own_tiles((0,), scale, sum_over_sites(done[-1], 1), yz)
+    sum_x, sum_yz = sum_over_sites(done[-1], part_yz)
+    return pl.pallas_call(
+        functools.partial(tiles_kernel, scale),
+        out_shape=jax.ShapeDtypeStruct((slots, 6 * TM * TM), F32),
+        in_specs=[vmem] * 3,
+        out_specs=vmem,
+        scratch_shapes=[pltpu.VMEM((modes, 6 * modes), BF16)],
+        compiler_params=small,
+        name="own_tiles",
+    )(own, sum_x, sum_yz)
 
 
 def solution(mesh):

time: 83.3 us -> 72.9 us (0.88)
  Pallas kernels: 71 us -> 60.2 us
    pallas_call x4 -> x3, Pallas kernels: 42.1 us -> 20.9 us  [the longest x1 17 us: sum_over_sites(): pl.pallas_call(functools.partial(sum_kernel, chips), out_shape=(jax.Shape...]
    pallas_call x2 -> x4, Pallas kernels: 10.3 us -> 15.9 us  [per_device(): pl.pallas_call(functools.partial(x_kernel, PARTS), out_shape=jax.ShapeDty...]
    pallas_call x1, Pallas kernels: 18.6 us -> 23.4 us  [per_device(): pl.pallas_call(yz_kernel, out_shape=(jax.ShapeDtypeStruct((8, half, half)...]
    ppermute x2 -> x4, starting transfers between devices: 6.25 us -> 6.98 us  [from_behind(): return lax.ppermute(block, axis, route)]
    transpose x3 -> x5, local copies, waits for them, and re-layouts: 4.78 us -> 4.36 us  [per_device(): eigvecs[j * part:(j + 1) * part].transpose(1, 2, 3, 0, 4)]
  transfers between devices with their start and end apart: 2 -> 4, of which waited for: 0 -> 0; matrix products, arithmetic and copies ran while one was open for 2% -> 2% of each run, Pallas kernels for 62% -> 51%
where the time goes in v3:
time: 72.9 us; the launch traced here: 72.6 us
  Pallas kernels  60.2 us (83%)
  starting transfers between devices  6.98 us (10%)
  local copies, waits for them, and re-layouts  5.24 us (7%)
    pallas_call x1, Pallas kernels, per_device(): pl.pallas_call(yz_kernel, out_shape=(jax.ShapeDtypeStruct((8, half, half)...  23.4 us
    pallas_call x1, Pallas kernels, sum_over_sites(): pl.pallas_call(functools.partial(sum_kernel, chips), out_shape=(jax.Shape...  17 us
    pallas_call x4, Pallas kernels, per_device(): pl.pallas_call(functools.partial(x_kernel, PARTS), out_shape=jax.ShapeDty...  15.9 us
    ppermute x4, starting transfers between devices, from_behind(): return lax.ppermute(block, axis, route)  6.98 us
    transpose x5, local copies, waits for them, and re-layouts, per_device(): eigvecs[j * part:(j + 1) * part].transpose(1, 2, 3, 0, 4)  4.36 us
    pallas_call x1, Pallas kernels, per_device(): pl.pallas_call(functools.partial(tiles_kernel, scale), out_shape=jax.Shap...  2.27 us
    pallas_call x1, Pallas kernels, sum_over_cores(): pl.pallas_call(core_sum_kernel, out_shape=jax.ShapeDtypeStruct(parts.shap...  1.64 us
  transfers between devices with their start and end apart: 4, of which 0 were waited for; matrix products, arithmetic and copies ran while one was open for 2% of the time, Pallas kernels for 51%

profile of v3, /device:TPU:0, one launch (start us, length us, event | category | flops | bytes accessed | tf_op | source)
XLA Modules:
  0.0 72.6 jit_solution(16491772108722314243)
XLA Ops:
  0.0 3.6 %slice_bitcast_fusion = (bf16[2,3,1,64,1024]{4,0,2,1,3:T(2,128)(2,1)S(1)}, bf16[2,3,1,64,1024]{4,0,2,1,3:T(2,128)(2,1)S(1)}, bf16[2,3,1,64,1024]{4,0,2,1,3:T(2,128)(2,1)S(1)}, bf16[2,3,1,64,1024]{4,0,2,1,3:T(2,128)(2,1)S(1)}) fusion(bf16[256,2,3,1,1024]{4,1,3,2,0:T(2,128)(2,1)} %param.3), kind=kLoop, calls=%fused_computation | loop fusion | bytes 6291456 | tf_op jit(solution)/shard_map/transpose | solution.py:417
  3.6 0.0 copy-start
  3.6 0.2 copy.10
  3.8 5.5 %collective-permute-start.3 = (bf16[6,64,1024]{2,1,0:T(8,128)(2,1)S(1)}, bf16[6,64,1024]{2,1,0:T(8,128)(2,1)}, u32[]{:S(2)}, u32[]{:S(2)}) collective-permute-start(bf16[6,64,1024]{2,1,0:T(8,128)(2,1)S(1)} %bitcast.17), channel_id=1, source_target_pairs={{1,0},{2,1},{3,2},{4,3},{5,4},{6,5},{7,6},{8,7},{9,8},{10,9},{11,1... | collective-permute-start | bytes 2359304 | tf_op jit(solution)/shard_map/ppermute | solution.py:27
  9.3 0.2 copy.8
  9.5 0.7 %collective-permute-start.1 = (bf16[6,64,1024]{2,1,0:T(8,128)(2,1)S(1)}, bf16[6,64,1024]{2,1,0:T(8,128)(2,1)}, u32[]{:S(2)}, u32[]{:S(2)}) collective-permute-start(bf16[6,64,1024]{2,1,0:T(8,128)(2,1)S(1)} %bitcast.23), channel_id=1, source_target_pairs={{1,0},{2,1},{3,2},{4,3},{5,4},{6,5},{7,6},{8,7},{9,8},{10,9},{11,1... | collective-permute-start | bytes 2359304 | tf_op jit(solution)/shard_map/ppermute | solution.py:27
  10.3 0.2 copy.9
  10.5 0.1 collective-permute-start.2
  10.5 0.2 copy.11
  10.7 0.7 collective-permute-start
  11.4 0.8 %dynamic_slice.3 = s32[130]{0:T(256)S(1)} dynamic-slice(s32[2080]{0:T(1024)} %param.5, s32[]{:T(128)S(6)} %select_n.3), dynamic_slice_sizes={130} | dynamic-slice | bytes 1044 | tf_op jit(solution)/shard_map/dynamic_slice | solution.py:422
  12.2 0.1 copy.12.slot_ref
  12.3 0.0 copy-done
  12.3 23.4 %products_yz.1 = (f32[8,128,128]{2,1,0:T(8,128)S(1)}, f32[1,18,8,128]{3,2,1,0:T(8,128)S(1)}) custom-call(s32[3]{0:T(128)S(1)} %copy-done, bf16[6,64,1024]{2,1,0:T(8,128)(2,1)S(1)} %bitcast.24, bf16[6,64,1024]{2,1,0:T(8,128)(2,1)S(1)} %bitcast.30, bf16[6,64,1024]{2,1,0:T(8,128)(2,1)S(1)} %bitcast.18, bf16[6,64,1024]{2,1,0:T(8,128)(2,1)S(1)} %bitcast.36), custom_call_target="tpu_custom_call" | custom-call | tf_op jit(solution)/shard_map/products_yz/pallas_call | solution.py:431
  35.7 1.6 %sum_over_cores.1.yz_ref = bf16[8,64,128]{2,1,0:T(8,128)(2,1)S(1)} custom-call(f32[2,8,64,128]{3,2,1,0:T(8,128)S(1)} %bitcast.42), custom_call_target="tpu_custom_call" | custom-call | tf_op jit(solution)/shard_map/sum_over_cores/pallas_call | solution.py:317
  37.4 0.0 collective-permute-done.3.refs_4_
  37.4 3.9 %products_x2.1.refs_7_ = f32[512,64]{1,0:T(8,128)S(1)} custom-call(f32[1,18,8,128]{3,2,1,0:T(8,128)S(1)} %get-tuple-element.9.ux_ref, bf16[6,64,1024]{2,1,0:T(8,128)(2,1)S(1)} %bitcast.25, bf16[6,64,1024]{2,1,0:T(8,128)(2,1)S(1)} %bitcast.31, bf16[6,64,1024]{2,1,0:T(8,128)(2,1)S(1)} %bitcast.19, bf16[6,64,1024]{2,1,0:T(8,128)(2,1)S(1)} %bitcast.37, ...), custom_call_target="tpu_custom_call" | custom-call | tf_op jit(solution)/shard_map/products_x2/pallas_call | solution.py:455
  41.3 0.0 collective-permute-done.1.refs_4_
  41.3 3.9 %products_x0.1.refs_5_ = f32[512,64]{1,0:T(8,128)S(1)} custom-call(f32[1,18,8,128]{3,2,1,0:T(8,128)S(1)} %get-tuple-element.9.ux_ref, bf16[6,64,1024]{2,1,0:T(8,128)(2,1)S(1)} %bitcast.26, bf16[6,64,1024]{2,1,0:T(8,128)(2,1)S(1)} %bitcast.32, bf16[6,64,1024]{2,1,0:T(8,128)(2,1)S(1)} %bitcast.20, bf16[6,64,1024]{2,1,0:T(8,128)(2,1)S(1)} %bitcast.38, ...), custom_call_target="tpu_custom_call" | custom-call | tf_op jit(solution)/shard_map/products_x0/pallas_call | solution.py:455
  45.3 0.0 collective-permute-done.2.refs_4_
  45.3 3.9 %products_x1.1.refs_6_ = f32[512,64]{1,0:T(8,128)S(1)} custom-call(f32[1,18,8,128]{3,2,1,0:T(8,128)S(1)} %get-tuple-element.9.ux_ref, bf16[6,64,1024]{2,1,0:T(8,128)(2,1)S(1)} %bitcast.27, bf16[6,64,1024]{2,1,0:T(8,128)(2,1)S(1)} %bitcast.33, bf16[6,64,1024]{2,1,0:T(8,128)(2,1)S(1)} %bitcast.21, bf16[6,64,1024]{2,1,0:T(8,128)(2,1)S(1)} %bitcast.39, ...), custom_call_target="tpu_custom_call" | custom-call | tf_op jit(solution)/shard_map/products_x1/pallas_call | solution.py:455
  49.2 0.0 collective-permute-done.refs_4_
  49.2 4.1 %products_x3.1 = f32[4,128,128]{2,1,0:T(8,128)S(1)} custom-call(f32[1,18,8,128]{3,2,1,0:T(8,128)S(1)} %get-tuple-element.9.ux_ref, bf16[6,64,1024]{2,1,0:T(8,128)(2,1)S(1)} %bitcast.28, bf16[6,64,1024]{2,1,0:T(8,128)(2,1)S(1)} %bitcast.34, bf16[6,64,1024]{2,1,0:T(8,128)(2,1)S(1)} %bitcast.22, bf16[6,64,1024]{2,1,0:T(8,128)(2,1)S(1)} %bitcast.40, ...), custom_call_target="tpu_custom_call" | custom-call | tf_op jit(solution)/shard_map/products_x3/pallas_call | solution.py:455
  53.3 17.0 %sum_over_sites.1 = (bf16[2,8,32,128]{3,2,1,0:T(8,128)(2,1)S(1)}, bf16[2,8,64,128]{3,2,1,0:T(8,128)(2,1)S(1)}) custom-call(f32[2,8,32,128]{3,2,1,0:T(8,128)S(1)} %bitcast.41, bf16[8,64,128]{2,1,0:T(8,128)(2,1)S(1)} %sum_over_cores.1.yz_ref), custom_call_target="tpu_custom_call" | custom-call | tf_op jit(solution)/shard_map/sum_over_sites/pallas_call | solution.py:339
  70.3 2.3 %own_tiles.1 = f32[130,96]{1,0:T(8,128)} custom-call(s32[130,1]{1,0:T(8,128)S(1)} %copy.12.slot_ref, bf16[4,128,128]{2,1,0:T(8,128)(2,1)S(1)} %bitcast.44, bf16[8,128,128]{2,1,0:T(8,128)(2,1)S(1)} %bitcast.43), custom_call_target="tpu_custom_call" | custom-call | tf_op jit(solution)/shard_map/own_tiles/pallas_call | solution.py:466
Async XLA Ops:
  3.6 8.7 %copy-start = (s32[3]{0:T(128)S(1)}, s32[3]{0:T(128)}, u32[]{:S(2)}) copy-start(s32[3]{0:T(128)} %seed_ref.1) | copy-start | bytes 40
  3.8 33.6 %collective-permute-start.3 = (bf16[6,64,1024]{2,1,0:T(8,128)(2,1)S(1)}, bf16[6,64,1024]{2,1,0:T(8,128)(2,1)}, u32[]{:S(2)}, u32[]{:S(2)}) collective-permute-start(bf16[6,64,1024]{2,1,0:T(8,128)(2,1)S(1)} %bitcast.17), channel_id=1, source_target_pairs={{1,0},{2,1},{3,2},{4,3},{5,4},{6,5},{7,6},{8,7},{9,8},{10,9},{11,1... | collective-permute-start | bytes 2359304 | tf_op jit(solution)/shard_map/ppermute | solution.py:27
  9.5 31.8 %collective-permute-start.1 = (bf16[6,64,1024]{2,1,0:T(8,128)(2,1)S(1)}, bf16[6,64,1024]{2,1,0:T(8,128)(2,1)}, u32[]{:S(2)}, u32[]{:S(2)}) collective-permute-start(bf16[6,64,1024]{2,1,0:T(8,128)(2,1)S(1)} %bitcast.23), channel_id=1, source_target_pairs={{1,0},{2,1},{3,2},{4,3},{5,4},{6,5},{7,6},{8,7},{9,8},{10,9},{11,1... | collective-permute-start | bytes 2359304 | tf_op jit(solution)/shard_map/ppermute | solution.py:27
  10.5 34.8 %collective-permute-start.2 = (bf16[6,64,1024]{2,1,0:T(8,128)(2,1)S(1)}, bf16[6,64,1024]{2,1,0:T(8,128)(2,1)}, u32[]{:S(2)}, u32[]{:S(2)}) collective-permute-start(bf16[6,64,1024]{2,1,0:T(8,128)(2,1)S(1)} %bitcast.29), channel_id=1, source_target_pairs={{1,0},{2,1},{3,2},{4,3},{5,4},{6,5},{7,6},{8,7},{9,8},{10,9},{11,1... | collective-permute-start | bytes 2359304 | tf_op jit(solution)/shard_map/ppermute | solution.py:27
  10.7 38.5 %collective-permute-start = (bf16[6,64,1024]{2,1,0:T(8,128)(2,1)S(1)}, bf16[6,64,1024]{2,1,0:T(8,128)(2,1)}, u32[]{:S(2)}, u32[]{:S(2)}) collective-permute-start(bf16[6,64,1024]{2,1,0:T(8,128)(2,1)S(1)} %bitcast.35), channel_id=1, source_target_pairs={{1,0},{2,1},{3,2},{4,3},{5,4},{6,5},{7,6},{8,7},{9,8},{10,9},{11,1... | collective-permute-start | bytes 2359304 | tf_op jit(solution)/shard_map/ppermute | solution.py:27

commit v4 on v3

--- a/solution.py
+++ b/solution.py
@@ -13,7 +13,7 @@
 MODULUS = 46337
 LANES = 128
 ROWS = 16
-PARTS = 4
+PARTS = 2
 LARGE = 32 * 1024 * 1024
 SMALL = 8 * 1024 * 1024
 MESH = pl.DeviceIdType.MESH

time: 72.9 us -> 70.1 us (0.962)
  Pallas kernels: 60.2 us -> 50.4 us
  waiting for transfers between devices: 0.01 us -> 7.41 us
  starting transfers between devices: 6.98 us -> 6.25 us
    ppermute x4 -> x2, waiting for transfers between devices: 0.01 us -> 7.41 us  [from_behind(): return lax.ppermute(block, axis, route)]
    pallas_call x4 -> x2, Pallas kernels: 15.9 us -> 10.3 us  [per_device(): pl.pallas_call(functools.partial(x_kernel, PARTS), out_shape=jax.ShapeDty...]
    pallas_call x1, Pallas kernels: 23.4 us -> 18.6 us  [per_device(): pl.pallas_call(yz_kernel, out_shape=(jax.ShapeDtypeStruct((8, half, half)...]
    ppermute x4 -> x2, starting transfers between devices: 6.98 us -> 6.25 us  [from_behind(): return lax.ppermute(block, axis, route)]
    transpose x5 -> x3, local copies, waits for them, and re-layouts: 4.36 us -> 4.78 us  [per_device(): eigvecs[j * part:(j + 1) * part].transpose(1, 2, 3, 0, 4)]
  transfers between devices with their start and end apart: 4 -> 2, of which waited for: 0 -> 1; matrix products, arithmetic and copies ran while one was open for 2% -> 2% of each run, Pallas kernels for 51% -> 36%
where the time goes in v4:
time: 70.1 us; the launch traced here: 69.8 us
  Pallas kernels  50.4 us (72%)
  waiting for transfers between devices  7.41 us (11%)
  starting transfers between devices  6.25 us (9%)
  local copies, waits for them, and re-layouts  5.66 us (8%)
    pallas_call x1, Pallas kernels, per_device(): pl.pallas_call(yz_kernel, out_shape=(jax.ShapeDtypeStruct((8, half, half)...  18.6 us
    pallas_call x1, Pallas kernels, sum_over_sites(): pl.pallas_call(functools.partial(sum_kernel, chips), out_shape=(jax.Shape...  17.7 us
    pallas_call x2, Pallas kernels, per_device(): pl.pallas_call(functools.partial(x_kernel, PARTS), out_shape=jax.ShapeDty...  10.3 us
    ppermute x2, waiting for transfers between devices, from_behind(): return lax.ppermute(block, axis, route)  7.41 us
    ppermute x2, starting transfers between devices, from_behind(): return lax.ppermute(block, axis, route)  6.25 us
    transpose x3, local copies, waits for them, and re-layouts, per_device(): eigvecs[j * part:(j + 1) * part].transpose(1, 2, 3, 0, 4)  4.78 us
    pallas_call x1, Pallas kernels, per_device(): pl.pallas_call(functools.partial(tiles_kernel, scale), out_shape=jax.Shap...  2.26 us
    pallas_call x1, Pallas kernels, sum_over_cores(): pl.pallas_call(core_sum_kernel, out_shape=jax.ShapeDtypeStruct(parts.shap...  1.62 us
  transfers between devices with their start and end apart: 2, of which 1 were waited for; matrix products, arithmetic and copies ran while one was open for 2% of the time, Pallas kernels for 36%

profile of v4, /device:TPU:0, one launch (start us, length us, event | category | flops | bytes accessed | tf_op | source)
XLA Modules:
  0.0 69.8 jit_solution(4512855440658363658)
XLA Ops:
  0.0 3.9 %slice_bitcast_fusion = (bf16[2,3,1,128,1024]{4,0,2,1,3:T(2,128)(2,1)S(1)}, bf16[2,3,1,128,1024]{4,0,2,1,3:T(2,128)(2,1)S(1)}) fusion(bf16[256,2,3,1,1024]{4,1,3,2,0:T(2,128)(2,1)} %param.3), kind=kLoop, calls=%fused_computation | loop fusion | bytes 6291456 | tf_op jit(solution)/shard_map/transpose | solution.py:417
  3.9 0.5 copy.6
  4.3 5.5 %collective-permute-start.1 = (bf16[6,128,1024]{2,1,0:T(8,128)(2,1)S(1)}, bf16[6,128,1024]{2,1,0:T(8,128)(2,1)}, u32[]{:S(2)}, u32[]{:S(2)}) collective-permute-start(bf16[6,128,1024]{2,1,0:T(8,128)(2,1)S(1)} %bitcast.11), channel_id=1, source_target_pairs={{1,0},{2,1},{3,2},{4,3},{5,4},{6,5},{7,6},{8,7},{9,8},{10,9},{11,1... | collective-permute-start | bytes 4718600 | tf_op jit(solution)/shard_map/ppermute | solution.py:27
  9.9 0.0 copy-start
  9.9 0.5 copy.7
  10.3 0.7 %collective-permute-start = (bf16[6,128,1024]{2,1,0:T(8,128)(2,1)S(1)}, bf16[6,128,1024]{2,1,0:T(8,128)(2,1)}, u32[]{:S(2)}, u32[]{:S(2)}) collective-permute-start(bf16[6,128,1024]{2,1,0:T(8,128)(2,1)S(1)} %bitcast.15), channel_id=1, source_target_pairs={{1,0},{2,1},{3,2},{4,3},{5,4},{6,5},{7,6},{8,7},{9,8},{10,9},{11,1... | collective-permute-start | bytes 4718600 | tf_op jit(solution)/shard_map/ppermute | solution.py:27
  11.1 0.8 %dynamic_slice.3 = s32[130]{0:T(256)S(1)} dynamic-slice(s32[2080]{0:T(1024)} %param.5, s32[]{:T(128)S(6)} %select_n.3), dynamic_slice_sizes={130} | dynamic-slice | bytes 1044 | tf_op jit(solution)/shard_map/dynamic_slice | solution.py:422
  11.8 0.1 copy.8.slot_ref
  11.9 0.0 copy-done
  12.0 18.6 %products_yz.1 = (f32[8,128,128]{2,1,0:T(8,128)S(1)}, f32[1,18,8,128]{3,2,1,0:T(8,128)S(1)}) custom-call(s32[3]{0:T(128)S(1)} %copy-done, bf16[6,128,1024]{2,1,0:T(8,128)(2,1)S(1)} %bitcast.12, bf16[6,128,1024]{2,1,0:T(8,128)(2,1)S(1)} %bitcast.16), custom_call_target="tpu_custom_call" | custom-call | tf_op jit(solution)/shard_map/products_yz/pallas_call | solution.py:431
  30.5 1.6 %sum_over_cores.1.yz_ref = bf16[8,64,128]{2,1,0:T(8,128)(2,1)S(1)} custom-call(f32[2,8,64,128]{3,2,1,0:T(8,128)S(1)} %bitcast.20), custom_call_target="tpu_custom_call" | custom-call | tf_op jit(solution)/shard_map/sum_over_cores/pallas_call | solution.py:317
  32.1 0.0 collective-permute-done.1.refs_2_
  32.2 5.1 %products_x0.1.refs_3_ = f32[512,128]{1,0:T(8,128)S(1)} custom-call(f32[1,18,8,128]{3,2,1,0:T(8,128)S(1)} %get-tuple-element.9.ux_ref, bf16[6,128,1024]{2,1,0:T(8,128)(2,1)S(1)} %bitcast.13, bf16[6,128,1024]{2,1,0:T(8,128)(2,1)S(1)} %bitcast.17, bf16[6,128,1024]{2,1,0:T(8,128)(2,1)} %collective-permute-done.1.refs_2_), custom_call_target="tpu_custom_call" | custom-call | tf_op jit(solution)/shard_map/products_x0/pallas_call | solution.py:455
  37.3 7.4 %collective-permute-done.refs_2_ = bf16[6,128,1024]{2,1,0:T(8,128)(2,1)} collective-permute-done((bf16[6,128,1024]{2,1,0:T(8,128)(2,1)S(1)}, bf16[6,128,1024]{2,1,0:T(8,128)(2,1)}, u32[]{:S(2)}, u32[]{:S(2)}) %collective-permute-start) | collective-permute-done | bytes 1572896 | tf_op jit(solution)/shard_map/ppermute | solution.py:27
  44.7 5.2 %products_x1.1 = f32[4,128,128]{2,1,0:T(8,128)S(1)} custom-call(f32[1,18,8,128]{3,2,1,0:T(8,128)S(1)} %get-tuple-element.9.ux_ref, bf16[6,128,1024]{2,1,0:T(8,128)(2,1)S(1)} %bitcast.14, bf16[6,128,1024]{2,1,0:T(8,128)(2,1)S(1)} %bitcast.18, bf16[6,128,1024]{2,1,0:T(8,128)(2,1)} %collective-permute-done.refs_2_, f32[512,128]{1,0:T(8,128)S(1)} %products_x0.1.refs_3_), custom_call_target="tpu_custom_call" | custom-call | tf_op jit(solution)/shard_map/products_x1/pallas_call | solution.py:455
  49.9 17.7 %sum_over_sites.1 = (bf16[2,8,32,128]{3,2,1,0:T(8,128)(2,1)S(1)}, bf16[2,8,64,128]{3,2,1,0:T(8,128)(2,1)S(1)}) custom-call(f32[2,8,32,128]{3,2,1,0:T(8,128)S(1)} %bitcast.19, bf16[8,64,128]{2,1,0:T(8,128)(2,1)S(1)} %sum_over_cores.1.yz_ref), custom_call_target="tpu_custom_call" | custom-call | tf_op jit(solution)/shard_map/sum_over_sites/pallas_call | solution.py:339
  67.6 2.3 %own_tiles.1 = f32[130,96]{1,0:T(8,128)} custom-call(s32[130,1]{1,0:T(8,128)S(1)} %copy.8.slot_ref, bf16[4,128,128]{2,1,0:T(8,128)(2,1)S(1)} %bitcast.22, bf16[8,128,128]{2,1,0:T(8,128)(2,1)S(1)} %bitcast.21), custom_call_target="tpu_custom_call" | custom-call | tf_op jit(solution)/shard_map/own_tiles/pallas_call | solution.py:466
Async XLA Ops:
  4.3 27.8 %collective-permute-start.1 = (bf16[6,128,1024]{2,1,0:T(8,128)(2,1)S(1)}, bf16[6,128,1024]{2,1,0:T(8,128)(2,1)}, u32[]{:S(2)}, u32[]{:S(2)}) collective-permute-start(bf16[6,128,1024]{2,1,0:T(8,128)(2,1)S(1)} %bitcast.11), channel_id=1, source_target_pairs={{1,0},{2,1},{3,2},{4,3},{5,4},{6,5},{7,6},{8,7},{9,8},{10,9},{11,1... | collective-permute-start | bytes 4718600 | tf_op jit(solution)/shard_map/ppermute | solution.py:27
  9.9 2.1 %copy-start = (s32[3]{0:T(128)S(1)}, s32[3]{0:T(128)}, u32[]{:S(2)}) copy-start(s32[3]{0:T(128)} %seed_ref.1) | copy-start | bytes 40
  10.3 34.3 %collective-permute-start = (bf16[6,128,1024]{2,1,0:T(8,128)(2,1)S(1)}, bf16[6,128,1024]{2,1,0:T(8,128)(2,1)}, u32[]{:S(2)}, u32[]{:S(2)}) collective-permute-start(bf16[6,128,1024]{2,1,0:T(8,128)(2,1)S(1)} %bitcast.15), channel_id=1, source_target_pairs={{1,0},{2,1},{3,2},{4,3},{5,4},{6,5},{7,6},{8,7},{9,8},{10,9},{11,1... | collective-permute-start | bytes 4718600 | tf_op jit(solution)/shard_map/ppermute | solution.py:27
